TPU v7x, 512 devices: a whole 4x8x8 slice. The times are simulated.
512 devices in a mesh: comp: 8 (over y), blk: 64 (over z, x, core).
Axes of the slice: x: 4, y: 8, z: 8, core: 2. Of those that a mesh axis runs over, the one named last changes fastest.
Arguments:
- base_state: float32 [8, 64, 6, 2, 128, 128], P('comp', 'blk'), may hold values from -1.2 to 5.2, as said below
- section_state: float32 [8, 64, 6, 2, 128, 128], P('comp', 'blk'), may hold values from -1.2 to 5.2, as said below
- volume: float32 [8, 64, 2, 128, 128], P('comp', 'blk'), may hold values from 0.25 to 12, as said below
- distance: float32 [8, 64, 2, 128, 128], P('comp', 'blk'), may hold values from 0.5 to 3
- orientation: int32 [8, 64, 3], replicated, may hold values from 0 to 1
Outputs:
- new_state: float32 [8, 64, 6, 2, 128, 128], P('comp', 'blk')
- residual_norm: float32 [], replicated
Inputs may be any that keep to these rules, and one draw needn't show every extreme that they name: `base_state`: a valid flow in every cell of every block: density between 0.6 and 1.4, pressure 0.4 (E - |m|^2 / (2 rho)) between 0.5 and 1.5, and a positive last field. `section_state`: a valid flow in every cell of every block, with the same bounds as base_state. `volume`: positive volumes.
All inputs are finite; a program needn't handle non-finite values.
Results may differ from a plain program's by a relative error of at most 0.0003.
Values sent between devices are 32-bit elements; how exact they have to be, the bound alone decides.
A program may use at most 64 MiB of HBM per device.

v0:
```python
import jax
import jax.numpy as jnp
from jax import lax
from jax.sharding import PartitionSpec as P

ADIABATIC_INDEX = 1.4
SENSOR_GAIN = 0.25
FOURTH_GAIN = 0.03125
VISCOSITY = 0.05
DIFFUSIVITY_QUOT = 0.72
DIFFUSE_SIGMA = 0.6666666666666666
PRODUCE_GAIN = 0.1355
DESTROY_GAIN = 3.239
DAMPING_CONST = 7.1
COURANT = 2.0
SECTION_WEIGHT = 0.5


def padded(cells, sides, width):
    for axis, dim in sides:
        count = lax.axis_size(axis)
        ends = count - 1
        head = lax.slice_in_dim(cells, 0, width, axis=dim)
        tail = lax.slice_in_dim(cells, cells.shape[dim] - width, cells.shape[dim], axis=dim)
        cells = jnp.concatenate(
            [
                lax.ppermute(tail, axis, [(i, (i + 1) % count) for i in range(ends)]),
                cells,
                lax.ppermute(head, axis, [((i + 1) % count, i) for i in range(ends)]),
            ],
            axis=dim,
        )
    return cells


def take_slab(array, axis, start, count):
    return lax.slice_in_dim(array, start, start + count, axis=axis)


def field_sign(count, field, dtype):
    return jnp.where(jnp.arange(count) == field, -1.0, 1.0).astype(dtype)[:, None, None, None]


def swap_fields(array, second, third):
    order = list(range(array.shape[0]))
    order[second] = third
    order[third] = second
    return jnp.stack([array[field] for field in order])


def reorient(layers, flags, second, third):
    count = layers.shape[0]
    result = jnp.where(
        flags[1] > 0, jnp.flip(layers, 2) * field_sign(count, second, layers.dtype), layers
    )
    result = jnp.where(
        flags[2] > 0, jnp.flip(result, 3) * field_sign(count, third, layers.dtype), result
    )
    turned = jnp.swapaxes(swap_fields(result, second, third), 2, 3)
    return jnp.where(flags[0] > 0, turned, result)


def restore(layers, flags, second, third):
    count = layers.shape[0]
    turned = jnp.swapaxes(swap_fields(layers, second, third), 2, 3)
    result = jnp.where(flags[0] > 0, turned, layers)
    result = jnp.where(
        flags[1] > 0, jnp.flip(result, 2) * field_sign(count, second, layers.dtype), result
    )
    result = jnp.where(
        flags[2] > 0, jnp.flip(result, 3) * field_sign(count, third, layers.dtype), result
    )
    return result


def assemble(own, below, above, flags_below, flags_above, first, last, second, third):
    depth = own.shape[1]
    lower = jnp.where(
        first,
        jnp.concatenate([own[:, :1], own[:, :1]], axis=1),
        reorient(below, flags_below, second, third),
    )
    upper = jnp.where(
        last,
        jnp.concatenate([own[:, depth - 1 :], own[:, depth - 1 :]], axis=1),
        restore(above, flags_above, second, third),
    )
    stacked = jnp.concatenate([lower, own, upper], axis=1)
    return jnp.pad(stacked, ((0, 0), (0, 0), (2, 2), (2, 2)), mode="edge")


def primitive(state):
    fluid_compactness = state[0:1]
    moment = state[1:4]
    velocity = moment / fluid_compactness
    thermodynamic_stress = (ADIABATIC_INDEX - 1.0) * (
        state[4:5]
        - 0.5
        * (moment[0:1] * velocity[0:1] + moment[1:2] * velocity[1:2] + moment[2:3] * velocity[2:3])
    )
    eddy_field = state[5:6] / fluid_compactness
    return jnp.concatenate([velocity, thermodynamic_stress, eddy_field], axis=0)


def total_speed(state, prims):
    sound = jnp.sqrt(ADIABATIC_INDEX * prims[3] / state[0])
    return jnp.abs(prims[0]) + sound + (jnp.abs(prims[1]) + sound) + (jnp.abs(prims[2]) + sound)


def crop_others(array, axis):
    for other in (1, 2, 3):
        if other != axis:
            array = take_slab(array, other, 2, array.shape[other] - 4)
    return array


def face_flux(state, prims, axis):
    state = crop_others(state, axis)
    prims = crop_others(prims, axis)
    count = state.shape[axis] - 4
    fluid_compactness = state[0:1]
    thermodynamic_stress = prims[3:4]
    normal = prims[axis - 1 : axis]
    speed = jnp.abs(normal) + jnp.sqrt(ADIABATIC_INDEX * thermodynamic_stress / fluid_compactness)
    fields = [state[field] * normal[0] for field in range(6)]
    fields[axis] = fields[axis] + thermodynamic_stress[0]
    fields[4] = fields[4] + thermodynamic_stress[0] * normal[0]
    inviscid = jnp.stack(fields)

    def interface_couple(array):
        return (take_slab(array, axis, 1, count + 1), take_slab(array, axis, 2, count + 1))

    flux_left, flux_right = interface_couple(inviscid)
    central = 0.5 * (flux_left + flux_right)
    before = take_slab(thermodynamic_stress, axis, 0, count + 2)
    middle = take_slab(thermodynamic_stress, axis, 1, count + 2)
    after = take_slab(thermodynamic_stress, axis, 2, count + 2)
    sensor = jnp.abs(after - 2.0 * middle + before) / (after + 2.0 * middle + before)
    second_gain = SENSOR_GAIN * jnp.maximum(
        take_slab(sensor, axis, 0, count + 1), take_slab(sensor, axis, 1, count + 1)
    )
    fourth_gain = jnp.maximum(0.0, FOURTH_GAIN - second_gain)
    speed_left, speed_right = interface_couple(speed)
    state_left, state_right = interface_couple(state)
    far_left = take_slab(state, axis, 0, count + 1)
    far_right = take_slab(state, axis, 3, count + 1)
    damping = (
        0.5
        * (speed_left + speed_right)
        * (
            second_gain * (state_right - state_left)
            - fourth_gain * (far_right - 3.0 * state_right + 3.0 * state_left - far_left)
        )
    )
    ratio_chi = state[5:6] / VISCOSITY
    cubed = ratio_chi * ratio_chi * ratio_chi
    eddy_viscosity = state[5:6] * cubed / (cubed + DAMPING_CONST * DAMPING_CONST * DAMPING_CONST)
    velocity = prims[0:3]
    kinetic = (
        velocity[0:1] * velocity[0:1]
        + velocity[1:2] * velocity[1:2]
        + velocity[2:3] * velocity[2:3]
    )
    control_volume_heat_level = thermodynamic_stress / fluid_compactness
    visc_left, visc_right = interface_couple(eddy_viscosity)
    interface_molecular_drag = VISCOSITY + 0.5 * (visc_left + visc_right)
    vel_left, vel_right = interface_couple(velocity)
    motion_energy_upwind, motion_energy_downwind = interface_couple(kinetic)
    thermal_state_upwind, thermal_state_downwind = interface_couple(control_volume_heat_level)
    turb_left, turb_right = interface_couple(state[5:6])
    nu_left, nu_right = interface_couple(prims[4:5])
    visc_moment = interface_molecular_drag * (vel_right - vel_left)
    dissipative_heat_flux = interface_molecular_drag * (
        0.5 * (motion_energy_downwind - motion_energy_upwind)
        + ADIABATIC_INDEX
        / ((ADIABATIC_INDEX - 1.0) * DIFFUSIVITY_QUOT)
        * (thermal_state_downwind - thermal_state_upwind)
    )
    visc_turb = (VISCOSITY + 0.5 * (turb_left + turb_right)) / DIFFUSE_SIGMA * (nu_right - nu_left)
    viscous = jnp.concatenate(
        [jnp.zeros_like(dissipative_heat_flux), visc_moment, dissipative_heat_flux, visc_turb],
        axis=0,
    )
    return central - damping - viscous


def slope(prims, field, axis):
    cropped = crop_others(prims[field : field + 1], axis)
    count = cropped.shape[axis] - 4
    return 0.5 * (take_slab(cropped, axis, 3, count) - take_slab(cropped, axis, 1, count))


def residual_terms(extended, wide_prims, cell_volume, wall_gap):
    flow = None
    for axis in (1, 2, 3):
        faces = face_flux(extended, wide_prims, axis)
        count = faces.shape[axis] - 1
        term = take_slab(faces, axis, 1, count) - take_slab(faces, axis, 0, count)
        flow = term if flow is None else flow + term
    inner = extended[:, 2:-2, 2:-2, 2:-2]
    spin_first = slope(wide_prims, 2, 2) - slope(wide_prims, 1, 3)
    spin_second = slope(wide_prims, 0, 3) - slope(wide_prims, 2, 1)
    spin_third = slope(wide_prims, 1, 1) - slope(wide_prims, 0, 2)
    spin = jnp.sqrt(
        jnp.square(spin_first) + jnp.square(spin_second) + jnp.square(spin_third) + 1e-06
    )
    eddy_field = wide_prims[4:5, 2:-2, 2:-2, 2:-2]
    source = PRODUCE_GAIN * spin * inner[5:6] - DESTROY_GAIN * inner[0:1] * jnp.square(
        eddy_field / wall_gap[None]
    )
    return jnp.concatenate([flow[:5], flow[5:6] - cell_volume[None] * source], axis=0)


def per_device(base_state, section_state, volume, distance, orientation):
    state = section_state[0, 0]
    cell_volume = volume[0, 0]
    wall_gap = distance[0, 0]
    depth = state.shape[1]
    group = lax.axis_index("comp")
    place = lax.axis_index("blk")
    chain = lax.axis_size("blk")
    own_prims = primitive(state)
    limit = jnp.min(cell_volume / total_speed(state, own_prims))
    smallest = lax.pmin(limit, ("comp", "blk"))
    table = lax.dynamic_index_in_dim(orientation, group, 0, keepdims=False)
    flags_below = lax.dynamic_index_in_dim(table, place, 0, keepdims=False)
    flags_above = lax.dynamic_index_in_dim(
        table, jnp.minimum(place + 1, chain - 1), 0, keepdims=False
    )
    first = place == 0
    last = place == chain - 1
    outgoing = jnp.concatenate([state, own_prims], axis=0)
    grown = padded(outgoing, (("blk", 1),), 2)
    extended = assemble(
        state, grown[:6, 0:2], grown[:6, depth + 2 :], flags_below, flags_above, first, last, 2, 3
    )
    wide_prims = assemble(
        own_prims,
        grown[6:, 0:2],
        grown[6:, depth + 2 :],
        flags_below,
        flags_above,
        first,
        last,
        1,
        2,
    )
    resid = residual_terms(extended, wide_prims, cell_volume, wall_gap)
    step = COURANT * smallest
    updated = base_state[0, 0] - SECTION_WEIGHT * step * resid / cell_volume[None]
    partial_value = jnp.sum(jnp.square(resid[0] / cell_volume))
    summed_terms = lax.psum(partial_value, ("comp", "blk"))
    cells = lax.axis_size("comp") * chain * depth * state.shape[2] * state.shape[3]
    return (updated[None, None], jnp.sqrt(summed_terms / cells))


def solution(mesh):
    placed = (
        P("comp", "blk", None, None, None, None),
        P("comp", "blk", None, None, None, None),
        P("comp", "blk", None, None, None),
        P("comp", "blk", None, None, None),
        P(),
    )
    return jax.shard_map(
        per_device,
        mesh=mesh,
        in_specs=placed,
        out_specs=(P("comp", "blk", None, None, None, None), P()),
        check_vma=False,
    )
```

profile of v0, /device:TPU:1, one launch (start us, length us, event | category | flops | bytes accessed | tf_op | source)
XLA Modules:
  0.0 348.2 jit_solution(8189842573898105592)
XLA Ops:
  2.7 1.9 broadcast_multiply_fusion
  5.8 4.5 %collective-permute-start = (f32[11,2,128,128]{3,2,1,0:T(8,128)}, f32[11,2,128,128]{3,2,1,0:T(8,128)}, u32[]{:S(2)}, u32[]{:S(2)}) collective-permute-start(f32[11,2,128,128]{3,2,1,0:T(8,128)} %pad_maximum_fusion.9), channel_id=1, source_target_pairs={{0,1},{1,2},{2,3},{3,4},{4,5},{5,6},{6,7},{7,8},{8,9},{9,10},{10,1... | collective-permute-start | bytes 4325384 | tf_op jit(solution)/shard_map/ppermute | solution.py:27
  10.3 6.7 %collective-permute-start.1 = (f32[11,2,128,128]{3,2,1,0:T(8,128)}, f32[11,2,128,128]{3,2,1,0:T(8,128)S(1)}, u32[]{:S(2)}, u32[]{:S(2)}) collective-permute-start(f32[11,2,128,128]{3,2,1,0:T(8,128)} %pad_maximum_fusion.9), channel_id=1, source_target_pairs={{1,0},{2,1},{3,2},{4,3},{5,4},{6,5},{7,6},{8,7},{9,8},{10,9},{11,1... | collective-permute-start | bytes 4325384 | tf_op jit(solution)/shard_map/ppermute | solution.py:29
  17.1 1.5 constant_dynamic-slice_fusion
  24.2 2.4 collective-permute-done
  27.7 3.2 rev.32
  36.9 3.2 rev.34
  40.1 1.7 multiply_select_fusion.5
  41.8 3.7 %rev.33 = f32[5,2,128,128]{3,2,1,0:T(8,128)} reverse(f32[5,2,128,128]{3,2,1,0:T(8,128)S(1)} %get-tuple-element.92), dimensions={3} | reverse | bytes 1310720 | tf_op jit(solution)/shard_map/jit(_flip)/rev | solution.py:57
  45.5 3.6 %rev.35 = f32[5,2,128,128]{3,2,1,0:T(8,128)} reverse(f32[5,2,128,128]{3,2,1,0:T(8,128)S(1)} %get-tuple-element.93), dimensions={3} | reverse | bytes 1310720 | tf_op jit(solution)/shard_map/jit(_flip)/rev | solution.py:71
  49.2 1.7 multiply_select_fusion.4
  53.8 3.9 %rev.28 = f32[6,2,128,128]{3,2,1,0:T(8,128)} reverse(f32[6,2,128,128]{3,2,1,0:T(8,128)S(1)} %slice.1052), dimensions={2} | reverse | bytes 1572864 | tf_op jit(solution)/shard_map/jit(_flip)/rev | solution.py:54
  62.2 3.8 %rev.30 = f32[6,2,128,128]{3,2,1,0:T(8,128)} reverse(f32[6,2,128,128]{3,2,1,0:T(8,128)S(1)} %slice_select_fusion), dimensions={2} | reverse | bytes 1572864 | tf_op jit(solution)/shard_map/jit(_flip)/rev | solution.py:68
  66.0 2.8 multiply_select_fusion.2
  68.8 4.4 %rev.29 = f32[6,2,128,128]{3,2,1,0:T(8,128)} reverse(f32[6,2,128,128]{3,2,1,0:T(8,128)S(1)} %get-tuple-element.88), dimensions={3} | reverse | bytes 1572864 | tf_op jit(solution)/shard_map/jit(_flip)/rev | solution.py:57
  73.1 7.2 %rev.31 = f32[6,2,128,128]{3,2,1,0:T(8,128)} reverse(f32[6,2,128,128]{3,2,1,0:T(8,128)} %get-tuple-element.89), dimensions={3} | reverse | bytes 1572864 | tf_op jit(solution)/shard_map/jit(_flip)/rev | solution.py:71
  80.3 1.7 multiply_select_fusion.1
  86.7 2.7 slice_reduce_fusion.2
  90.6 8.1 %pad_maximum_fusion.1 = (f32[5,6,132,130]{3,2,1,0:T(8,128)}, f32[5,6,132,130]{3,2,1,0:T(8,128)}) fusion(f32[5,6,132,2]{3,2,1,0:T(8,128)S(1)} %reshape.207, f32[5,6,2,128]{3,2,1,0:T(2,128)S(1)} %reshape.203, f32[5,2,128,128]{3,2,1,0:T(8,128)S(1)} %get-tuple-element.91, f32[1,2,128,128]{3,2,1,0:T(8,128)S(1)} %get-tuple-element.57, ...), kind=kLoop, calls=%fused_computation.1 | loop fusion | flops 7207200 | bytes 6209280 | tf_op jit(solution)/shard_map/jit(_pad)/concatenate | solution.py:89
  98.7 7.3 %pad_maximum_fusion = f32[5,6,132,132]{3,2,1,0:T(8,128)} fusion(f32[5,6,132,2]{3,2,1,0:T(8,128)S(1)} %reshape.207, f32[5,6,2,128]{3,2,1,0:T(2,128)S(1)} %reshape.203, f32[5,2,128,128]{3,2,1,0:T(8,128)S(1)} %get-tuple-element.91, f32[1,2,128,128]{3,2,1,0:T(8,128)S(1)} %get-tuple-element.57, f32[1,2,128,128]{3,2,1,0:T(8,128)S(1)} %get-tuple-element.22, ...), kind=kLoop, calls=%fused_computation | loop fusion | flops 4181760 | bytes 4181760 | tf_op jit(solution)/shard_map/jit(_pad)/concatenate | solution.py:89
  105.9 1.8 copy.158
  107.8 1.7 copy.157
  109.4 1.6 copy.156
  111.1 1.8 copy.155
  112.9 1.7 maximum_select_fusion
  114.9 3.2 slice_reduce_fusion
  126.2 1.7 fusion.28
  129.8 6.0 %fusion.4 = f32[6,2,128,129]{3,2,1,0:T(8,128)S(1)} fusion(f32[6,6,132,2]{3,2,1,0:T(8,128)S(1)} %reshape.204, f32[6,6,2,128]{3,2,1,0:T(2,128)S(1)} %reshape.201, f32[6,6,2,128]{3,2,1,0:T(2,128)S(1)} %reshape.200, f32[6,2,128,128]{3,2,1,0:T(8,128)S(1)} %get-tuple-element.87, f32[6,2,128,128]{3,2,1,0:T(8,128)S(1)} %bitcast.168, ...), kind=kLoop, calls=%fused_computation.26 | loop fusion | flops 7331328 | bytes 6075648 | tf_op jit(solution)/shard_map/sub | solution.py:184
  139.2 2.2 fusion.114
  142.1 105.8 %pmin.7 = f32[]{:T(128)} all-reduce(f32[]{:T(128)} %get-tuple-element.11), channel_id=1, replica_groups=mesh['comp'=8,'blk'=64] {'comp','blk'}, use_global_device_ids=true, to_apply=%region_1.0 | all-reduce | flops 1 | bytes 8 | tf_op jit(solution)/shard_map/pmin | solution.py:224
  247.9 95.4 %psum.7 = f32[]{:T(128)} all-reduce(f32[]{:T(128)} %get-tuple-element.10), channel_id=1, replica_groups=mesh['comp'=8,'blk'=64] {'comp','blk'}, use_global_device_ids=true, to_apply=%region_3.4 | all-reduce | flops 1 | bytes 8 | tf_op jit(solution)/shard_map/psum | solution.py:252
  344.0 3.1 fusion.32
  (136 shorter events, 39.5 us)
Async XLA Ops:
  0.6 4.0 %copy-start = (f32[1,1,6,2,128,128]{5,4,3,2,1,0:T(8,128)S(1)}, f32[1,1,6,2,128,128]{5,4,3,2,1,0:T(8,128)}, u32[]{:S(2)}) copy-start(f32[1,1,6,2,128,128]{5,4,3,2,1,0:T(8,128)} %param.6) | copy-start | bytes 2359300
  5.8 20.8 %collective-permute-start = (f32[11,2,128,128]{3,2,1,0:T(8,128)}, f32[11,2,128,128]{3,2,1,0:T(8,128)}, u32[]{:S(2)}, u32[]{:S(2)}) collective-permute-start(f32[11,2,128,128]{3,2,1,0:T(8,128)} %pad_maximum_fusion.9), channel_id=1, source_target_pairs={{0,1},{1,2},{2,3},{3,4},{4,5},{5,6},{6,7},{7,8},{8,9},{9,10},{10,1... | collective-permute-start | bytes 4325384 | tf_op jit(solution)/shard_map/ppermute | solution.py:27
  10.3 20.6 %collective-permute-start.1 = (f32[11,2,128,128]{3,2,1,0:T(8,128)}, f32[11,2,128,128]{3,2,1,0:T(8,128)S(1)}, u32[]{:S(2)}, u32[]{:S(2)}) collective-permute-start(f32[11,2,128,128]{3,2,1,0:T(8,128)} %pad_maximum_fusion.9), channel_id=1, source_target_pairs={{1,0},{2,1},{3,2},{4,3},{5,4},{6,5},{7,6},{8,7},{9,8},{10,9},{11,1... | collective-permute-start | bytes 4325384 | tf_op jit(solution)/shard_map/ppermute | solution.py:29
  31.0 4.8 %copy-start.6 = (f32[11,2,128,128]{3,2,1,0:T(8,128)}, f32[11,2,128,128]{3,2,1,0:T(8,128)S(1)}, u32[]{:S(2)}) copy-start(f32[11,2,128,128]{3,2,1,0:T(8,128)S(1)} %collective-permute-done.1) | copy-start | bytes 4325380
  50.9 0.9 copy-start.5
  51.8 5.9 %copy-start.14 = (f32[2,2,128,128]{3,2,1,0:T(8,128)S(1)}, f32[2,2,128,128]{3,2,1,0:T(8,128)}, u32[]{:S(2)}) copy-start(f32[2,2,128,128]{3,2,1,0:T(8,128)} %get-tuple-element.43) | copy-start | bytes 786436
  51.8 5.9 %copy-start.15 = (f32[2,2,128,128]{3,2,1,0:T(8,128)S(1)}, f32[2,2,128,128]{3,2,1,0:T(8,128)}, u32[]{:S(2)}) copy-start(f32[2,2,128,128]{3,2,1,0:T(8,128)} %get-tuple-element.45) | copy-start | bytes 786436
  51.8 5.9 %copy-start.16 = (f32[1,2,128,128]{3,2,1,0:T(8,128)S(1)}, f32[1,2,128,128]{3,2,1,0:T(8,128)}, u32[]{:S(2)}) copy-start(f32[1,2,128,128]{3,2,1,0:T(8,128)} %get-tuple-element.46) | copy-start | bytes 393220
  61.3 0.9 copy-start.4
  68.8 11.5 %copy-start.3 = (f32[6,2,128,128]{3,2,1,0:T(8,128)}, f32[6,2,128,128]{3,2,1,0:T(8,128)S(1)}, u32[]{:S(2)}) copy-start(f32[6,2,128,128]{3,2,1,0:T(8,128)S(1)} %get-tuple-element.88) | copy-start | bytes 2359300
  68.8 11.5 %copy-start.11 = (f32[6,1,128,128]{3,2,1,0:T(8,128)S(1)}, f32[6,1,128,128]{3,2,1,0:T(8,128)}, u32[]{:S(2)}) copy-start(f32[6,1,128,128]{3,2,1,0:T(8,128)} %get-tuple-element.56) | copy-start | bytes 1179652
  80.3 3.6 %copy-start.13 = (f32[2,2,128,128]{3,2,1,0:T(8,128)S(1)}, f32[2,2,128,128]{3,2,1,0:T(8,128)}, u32[]{:S(2)}) copy-start(f32[2,2,128,128]{3,2,1,0:T(8,128)} %slice.1069) | copy-start | bytes 786436
  80.3 3.6 %copy-start.18 = (f32[1,2,128,128]{3,2,1,0:T(8,128)S(1)}, f32[1,2,128,128]{3,2,1,0:T(8,128)}, u32[]{:S(2)}) copy-start(f32[1,2,128,128]{3,2,1,0:T(8,128)} %get-tuple-element.60) | copy-start | bytes 393220
  80.3 3.5 %copy-start.19 = (f32[1,2,128,128]{3,2,1,0:T(8,128)S(1)}, f32[1,2,128,128]{3,2,1,0:T(8,128)}, u32[]{:S(2)}) copy-start(f32[1,2,128,128]{3,2,1,0:T(8,128)} %get-tuple-element.61) | copy-start | bytes 393220
  80.3 3.5 %copy-start.20 = (f32[1,2,128,128]{3,2,1,0:T(8,128)S(1)}, f32[1,2,128,128]{3,2,1,0:T(8,128)}, u32[]{:S(2)}) copy-start(f32[1,2,128,128]{3,2,1,0:T(8,128)} %get-tuple-element.62) | copy-start | bytes 393220
  82.1 1.1 copy-start.2
  86.5 12.2 %copy-start.7 = (f32[5,6,2,128]{3,2,1,0:T(2,128)}, f32[5,6,2,128]{3,2,1,0:T(2,128)S(1)}, u32[]{:S(2)}) copy-start(f32[5,6,2,128]{3,2,1,0:T(2,128)S(1)} %reshape.202) | copy-start | bytes 92164
  86.5 12.2 %copy-start.9 = (f32[5,6,2,128]{3,2,1,0:T(2,128)}, f32[5,6,2,128]{3,2,1,0:T(2,128)S(1)}, u32[]{:S(2)}) copy-start(f32[5,6,2,128]{3,2,1,0:T(2,128)S(1)} %reshape.203) | copy-start | bytes 92164
  118.1 2.2 copy-start.1
  123.0 0.8 copy-start.8
  123.0 0.8 copy-start.10
  137.8 1.3 copy-start.12
  137.8 1.3 copy-start.21
  139.2 2.2 copy-start.17
where the time goes:
time: 350 us; the launch traced here: 348 us
  blocking collectives  201 us (57%)
  local copies, waits for them, and re-layouts  68.5 us (20%)
  other arithmetic  58.1 us (17%)
  starting transfers between devices  11.2 us (3%)
  between operations  6.85 us (2%)
    pmin x1, blocking collectives, per_device(): smallest = lax.pmin(limit, ('comp', 'blk'))  106 us
    psum x1, blocking collectives, per_device(): summed_terms = lax.psum(partial_value, ('comp', 'blk'))  95.4 us
    concatenate x5, other arithmetic, assemble(): return jnp.pad(stacked, ((0, 0), (0, 0), (2, 2), (2, 2)), mode='edge')  16.2 us
    unnamed x54, local copies, waits for them, and re-layouts  12.3 us
    rev x2, local copies, waits for them, and re-layouts, restore(): jnp.flip(result, 3) * field_sign(count, third, layers.dtype)  10.8 us
    rev x2, local copies, waits for them, and re-layouts, reorient(): jnp.flip(result, 3) * field_sign(count, third, layers.dtype)  8.06 us
    sub x3, other arithmetic, face_flux(): return central - damping - viscous  7.91 us
    rev x2, local copies, waits for them, and re-layouts, reorient(): jnp.flip(layers, 2) * field_sign(count, second, layers.dtype)  7.12 us
  transfers between devices with their start and end apart: 2, of which 1 were waited for; matrix products, arithmetic and copies ran while one was open for 2% of the time, Pallas kernels for 0%

commit v1 on v0

v1 whole, which is shorter than its diff:
```python
import functools

import jax
import jax.numpy as jnp
from jax import lax
from jax.experimental import pallas as pl
from jax.experimental.pallas import tpu as pltpu
from jax.sharding import PartitionSpec as P

GAMMA = 1.4
HEAT = 1.4 / (0.4 * 0.72)
CUBE = 7.1 * 7.1 * 7.1
MESH = pl.DeviceIdType.MESH
VMEM = pltpu.VMEM
FACE = 128
PAD = 8


def primitives(w):
    inv = 1.0 / w[0]
    u = [w[1] * inv, w[2] * inv, w[3] * inv]
    kinetic = 0.5 * (w[1] * u[0] + w[2] * u[1] + w[3] * u[2])
    p = 0.4 * (w[4] - kinetic)
    heat = p * inv
    cs = jnp.sqrt(GAMMA * heat)
    chi = w[5] * 20.0
    cubed = chi * chi * chi
    mu = w[5] * cubed / (cubed + CUBE)
    h = 0.5 * (u[0] * u[0] + u[1] * u[1] + u[2] * u[2]) + HEAT * heat
    return {"u": u, "p": p, "cs": cs, "mu": mu, "h": h, "nu": w[5] * inv}


def sensor(before, middle, after):
    twice = 2.0 * middle
    total = after + before
    return jnp.abs(total - twice) / (total + twice)


def face_flux(a, wm, w0, w1, w2, q0, q1, s0, s1, fields=range(6)):
    un0, un1 = q0["u"][a - 1], q1["u"][a - 1]
    half = 0.5 * ((jnp.abs(un0) + q0["cs"]) + (jnp.abs(un1) + q1["cs"]))
    e2 = 0.25 * jnp.maximum(s0, s1)
    e4 = jnp.maximum(0.0, 0.03125 - e2)
    b = half * e4
    c = half * e2 + 3.0 * b
    h0, h1 = 0.5 * un0, 0.5 * un1
    muf = 0.05 + 0.5 * (q0["mu"] + q1["mu"])
    out = []
    for f in fields:
        c0, c1 = w0[f], w1[f]
        if f == 4:
            c0, c1 = c0 + q0["p"], c1 + q1["p"]
        g = c0 * h0 + c1 * h1
        if f == a:
            g = g + 0.5 * (q0["p"] + q1["p"])
        g = g - c * (w1[f] - w0[f]) + b * (w2[f] - wm[f])
        if 1 <= f <= 3:
            g = g - muf * (q1["u"][f - 1] - q0["u"][f - 1])
        elif f == 4:
            g = g - muf * (q1["h"] - q0["h"])
        elif f == 5:
            g = g - (0.075 + 0.75 * (w0[5] + w1[5])) * (q1["nu"] - q0["nu"])
        out.append(g)
    return out


def edge_flux(a, w0, w1, q0, s0):
    un = q0["u"][a - 1]
    b = (jnp.abs(un) + q0["cs"]) * jnp.maximum(0.0, 0.03125 - 0.25 * s0)
    out = []
    for f in range(6):
        c0 = w0[f] + q0["p"] if f == 4 else w0[f]
        g = c0 * un
        if f == a:
            g = g + q0["p"]
        out.append(g + b * (w1[f] - w0[f]))
    return out


NAMES = ("u0", "u1", "u2", "p", "cs", "mu", "h", "nu")


def local_kernel(state, volume, part, vort, limit, wide):
    rows = 8

    for layer in range(2):

        def fill(k, least):
            at = pl.ds(pl.multiple_of(k * rows, rows), rows)
            to = pl.ds(pl.multiple_of(k * rows + PAD, rows), rows)
            w = [state[f, layer, at, :] for f in range(6)]
            q = primitives(w)
            u = q["u"]
            for f in range(6):
                wide[f, layer, to, :] = w[f]
            for i, x in enumerate(u + [q["p"], q["cs"], q["mu"], q["h"], q["nu"]]):
                wide[6 + i, layer, to, :] = x
            speed = (jnp.abs(u[0]) + q["cs"]) + (jnp.abs(u[1]) + q["cs"]) + (jnp.abs(u[2]) + q["cs"])
            return jnp.minimum(least, volume[layer, at, :] / speed)

        start = jnp.full((rows, FACE), jnp.inf, jnp.float32) if layer == 0 else limit[...]
        limit[...] = lax.fori_loop(0, FACE // rows, fill, start)
        for i in range(14):
            head = wide[i, layer, PAD : PAD + 1, :]
            tail = wide[i, layer, PAD + FACE - 1 : PAD + FACE, :]
            wide[i, layer, PAD - 2 : PAD - 1, :] = head
            wide[i, layer, PAD - 1 : PAD, :] = head
            wide[i, layer, PAD + FACE : PAD + FACE + 1, :] = tail
            wide[i, layer, PAD + FACE + 1 : PAD + FACE + 2, :] = tail

    lane = lax.broadcasted_iota(jnp.int32, (rows, FACE), 1)
    row = lax.broadcasted_iota(jnp.int32, (rows, FACE), 0)
    first, last, top = lane == 0, lane == FACE - 1, row == 0

    def after(x):
        return jnp.where(last, x, pltpu.roll(x, FACE - 1, 1))

    def before(x):
        return jnp.where(first, x, pltpu.roll(x, 1, 1))

    for layer in range(2):

        def load(i, k, offset):
            return wide[i, layer, pl.ds(k * rows + PAD + offset, rows), :]

        def cell(k, offset):
            v = [load(6 + i, k, offset) for i in range(8)]
            return {"u": v[:3], "p": v[3], "cs": v[4], "mu": v[5], "h": v[6], "nu": v[7]}

        def states(k, offset):
            return [load(f, k, offset) for f in range(6)]

        def body(k, carry):
            w0, q0 = states(k, 0), cell(k, 0)
            w1, q1 = states(k, 1), cell(k, 1)
            pm, p2 = load(9, k, -1), load(9, k, 2)
            s0 = sensor(pm, q0["p"], q1["p"])
            s1 = sensor(q0["p"], q1["p"], p2)
            g = face_flux(2, states(k, -1), w0, w1, states(k, 2), q0, q1, s0, s1)
            turned = [pltpu.roll(x, 1, 0) for x in g]
            total = [x - jnp.where(top, c, y) for x, y, c in zip(g, turned, carry)]
            d2u0 = 0.5 * (q1["u"][0] - load(6, k, -1))
            d2u2 = 0.5 * (q1["u"][2] - load(8, k, -1))
            w1 = [after(x) for x in w0]
            w2 = [after(x) for x in w1]
            wm = [before(x) for x in w0]
            q1 = {n: after(q0[n]) for n in ("p", "cs", "mu", "h", "nu")}
            q1["u"] = [after(x) for x in q0["u"]]
            s0 = sensor(before(q0["p"]), q0["p"], q1["p"])
            g = face_flux(3, wm, w0, w1, w2, q0, q1, s0, after(s0))
            edge = edge_flux(3, w0, w1, q0, s0)
            total = [
                t + (x - jnp.where(first, e, pltpu.roll(x, 1, 1)))
                for t, x, e in zip(total, g, edge)
            ]
            d3u0 = 0.5 * (q1["u"][0] - before(q0["u"][0]))
            d3u1 = 0.5 * (q1["u"][1] - before(q0["u"][1]))
            at = pl.ds(pl.multiple_of(k * rows, rows), rows)
            for f in range(6):
                part[f, layer, at, :] = total[f]
            vort[0, layer, at, :] = d2u2 - d3u1
            vort[1, layer, at, :] = d3u0
            vort[2, layer, at, :] = d2u0
            return tuple(turned)

        w0, q0 = states(0, 0), cell(0, 0)
        p1 = load(9, 0, 1)
        init = edge_flux(2, w0, states(0, 1), q0, sensor(load(9, 0, -1), q0["p"], p1))
        lax.fori_loop(0, FACE // rows, body, tuple(init))


def chain_kernel(
    flags, least, state, base, volume, distance, part, vort, below, above, new, acc, low, high
):
    rows = 8
    steps = FACE // rows
    lane = lax.broadcasted_iota(jnp.int32, (rows, FACE), 1)
    row = lax.broadcasted_iota(jnp.int32, (rows, FACE), 0)

    def ghosts(source, target, turn, flip_rows, flip_lanes, sign2, sign3):
        lanes = jnp.where(flip_lanes > 0, FACE - 1 - lane, lane)
        rowi = jnp.where(flip_rows > 0, rows - 1 - row, row)

        def place(read):
            def body(k, _):
                kk = jnp.where(flip_rows > 0, steps - 1 - k, k)
                at = pl.ds(pl.multiple_of(kk * rows, rows), rows)
                to = pl.ds(pl.multiple_of(k * rows, rows), rows)
                for f in range(6):
                    for layer in range(2):
                        x = read(f, layer, at)
                        x = jnp.take_along_axis(x, lanes, axis=1)
                        x = jnp.take_along_axis(x, rowi, axis=0)
                        if f == 2:
                            x = x * sign2
                        if f == 3:
                            x = x * sign3
                        target[f, layer, to, :] = x
                return 0

            lax.fori_loop(0, steps, body, 0)

        @pl.when(turn > 0)
        def _():
            for f in range(6):
                g = {2: 3, 3: 2}.get(f, f)
                for layer in range(2):
                    new[f, layer] = source[g, layer].T
            place(lambda f, layer, at: new[f, layer, at, :])

        @pl.when(turn == 0)
        def _():
            place(lambda f, layer, at: source[f, layer, at, :])

    is_first, is_last = flags[6], flags[7]

    @pl.when(is_first > 0)
    def _():
        for f in range(6):
            for layer in range(2):
                low[f, layer] = state[f, 0]

    @pl.when(is_first == 0)
    def _():
        t, r2, r3 = flags[0], flags[1], flags[2]
        s2 = 1.0 - 2.0 * jnp.where(t > 0, r3, r2).astype(jnp.float32)
        s3 = 1.0 - 2.0 * jnp.where(t > 0, r2, r3).astype(jnp.float32)
        ghosts(below, low, t, jnp.where(t > 0, r3, r2), jnp.where(t > 0, r2, r3), s2, s3)

    @pl.when(is_last > 0)
    def _():
        for f in range(6):
            for layer in range(2):
                high[f, layer] = state[f, 1]

    @pl.when(is_last == 0)
    def _():
        t, r2, r3 = flags[3], flags[4], flags[5]
        s2 = 1.0 - 2.0 * r2.astype(jnp.float32)
        s3 = 1.0 - 2.0 * r3.astype(jnp.float32)
        ghosts(above, high, t, r2, r3, s2, s3)

    smallest = least[0, 0]

    def body(k, total):
        at = pl.ds(pl.multiple_of(k * rows, rows), rows)
        w = []
        for ref, layer in ((low, 0), (low, 1), (state, 0), (state, 1), (high, 0), (high, 1)):
            w.append([ref[f, layer, at, :] for f in range(6)])
        q = [primitives(x) for x in w]
        s = [None] + [sensor(q[i - 1]["p"], q[i]["p"], q[i + 1]["p"]) for i in range(1, 5)]
        g = [
            face_flux(1, w[i - 1], w[i], w[i + 1], w[i + 2], q[i], q[i + 1], s[i], s[i + 1])
            for i in range(1, 4)
        ]
        for layer in range(2):
            i = layer + 2
            vol = volume[layer, at, :]
            inv = 1.0 / vol
            scale = smallest * inv
            d1u1 = 0.5 * (q[i + 1]["u"][1] - q[i - 1]["u"][1])
            d1u2 = 0.5 * (q[i + 1]["u"][2] - q[i - 1]["u"][2])
            w1 = vort[0, layer, at, :]
            w2 = vort[1, layer, at, :] - d1u2
            w3 = d1u1 - vort[2, layer, at, :]
            spin = jnp.sqrt(w1 * w1 + w2 * w2 + w3 * w3 + 1e-6)
            ratio = q[i]["nu"] / distance[layer, at, :]
            source = 0.1355 * spin * w[i][5] - 3.239 * w[i][0] * (ratio * ratio)
            for f in range(6):
                r = part[f, layer, at, :] + (g[layer + 1][f] - g[layer][f])
                if f == 5:
                    r = r - vol * source
                if f == 0:
                    z = r * inv
                    total = total + z * z
                new[f, layer, at, :] = base[f, layer, at, :] - scale * r
        return total

    acc[...] = lax.fori_loop(0, steps, body, jnp.zeros((rows, FACE), jnp.float32))


def reduce_kernel(op, value, out, slots, send, recv):
    comp, blk = lax.axis_index("comp"), lax.axis_index("blk")
    low, high = blk % 8, blk // 8
    phases = (
        (low, lambda j: (comp, high * 8 + j)),
        (comp, lambda j: (j, blk)),
        (high, lambda j: (comp, j * 8 + low)),
    )
    barrier = pltpu.get_barrier_semaphore()
    for me, device in phases:
        for step in range(1, 8):
            pl.semaphore_signal(
                barrier, inc=1, device_id=device((me + step) % 8), device_id_type=MESH
            )
    pl.semaphore_wait(barrier, 21)
    held = value[...]
    for n, (me, device) in enumerate(phases):
        slots[n, pl.ds(me, 1)] = held[None]
        copies = []
        for step in range(1, 8):
            copy = pltpu.make_async_remote_copy(
                src_ref=slots.at[n, me],
                dst_ref=slots.at[n, me],
                send_sem=send.at[n, step],
                recv_sem=recv.at[n, me],
                device_id=device((me + step) % 8),
                device_id_type=MESH,
            )
            copy.start()
            copies.append(copy)
        for step in range(1, 8):
            other = (me + step) % 8
            pltpu.make_async_remote_copy(
                src_ref=slots.at[n, me],
                dst_ref=slots.at[n, other],
                send_sem=send.at[n, step],
                recv_sem=recv.at[n, other],
                device_id=device(other),
                device_id_type=MESH,
            ).wait_recv()
        held = slots[n, 0]
        for j in range(1, 8):
            held = jnp.minimum(held, slots[n, j]) if op == "min" else held + slots[n, j]
        for copy in copies:
            copy.wait_send()
    if op == "min":
        out[...] = jnp.min(held, axis=(0, 1), keepdims=True)
    else:
        out[...] = jnp.sum(held, axis=(0, 1), keepdims=True)


def reduce_all(op, value, collective_id):
    return pl.pallas_call(
        functools.partial(reduce_kernel, op),
        out_shape=jax.ShapeDtypeStruct((1, 1), jnp.float32),
        in_specs=[pl.BlockSpec(memory_space=VMEM)],
        out_specs=pl.BlockSpec(memory_space=VMEM),
        scratch_shapes=[
            VMEM((3, 8, 8, FACE), jnp.float32),
            pltpu.SemaphoreType.DMA((3, 8)),
            pltpu.SemaphoreType.DMA((3, 8)),
        ],
        compiler_params=pltpu.CompilerParams(collective_id=collective_id, has_side_effects=True),
        cost_estimate=pl.CostEstimate(flops=1000, bytes_accessed=2**20, transcendentals=0),
        name="reduce_" + op,
    )(value)


def per_device(base_state, section_state, volume, distance, orientation):
    state, base = section_state[0, 0], base_state[0, 0]
    vol, gap = volume[0, 0], distance[0, 0]
    group, place = lax.axis_index("comp"), lax.axis_index("blk")
    chain = lax.axis_size("blk")
    f32 = functools.partial(jax.ShapeDtypeStruct, dtype=jnp.float32)
    vm = pl.BlockSpec(memory_space=VMEM)
    sm = pl.BlockSpec(memory_space=pltpu.SMEM)
    plane = (2, FACE, FACE)

    below = lax.ppermute(state, "blk", [(i, i + 1) for i in range(chain - 1)])
    above = lax.ppermute(state, "blk", [(i + 1, i) for i in range(chain - 1)])

    part, vort, limit = pl.pallas_call(
        local_kernel,
        out_shape=(f32((6,) + plane), f32((3,) + plane), f32((8, FACE))),
        in_specs=[vm, vm],
        out_specs=(vm, vm, vm),
        scratch_shapes=[VMEM((14, 2, FACE + 2 * PAD, FACE), jnp.float32)],
        cost_estimate=pl.CostEstimate(
            flops=40_000_000, bytes_accessed=3_000_000, transcendentals=400_000
        ),
        name="local_flux",
    )(state, vol)
    least = reduce_all("min", limit, 1)

    table = lax.dynamic_index_in_dim(orientation, group, 0, keepdims=False)
    mine = lax.dynamic_index_in_dim(table, place, 0, keepdims=False)
    after = lax.dynamic_index_in_dim(table, jnp.minimum(place + 1, chain - 1), 0, keepdims=False)
    ends = jnp.stack([place == 0, place == chain - 1]).astype(jnp.int32)
    flags = jnp.concatenate([mine, after, ends])

    new, acc = pl.pallas_call(
        chain_kernel,
        out_shape=(f32((6,) + plane), f32((8, FACE))),
        in_specs=[sm, sm] + [vm] * 8,
        out_specs=(vm, vm),
        scratch_shapes=[VMEM((6,) + plane, jnp.float32)] * 2,
        cost_estimate=pl.CostEstimate(
            flops=40_000_000, bytes_accessed=5_000_000, transcendentals=400_000
        ),
        name="chain_flux",
    )(flags, least, state, base, vol, gap, part, vort, below, above)
    total = reduce_all("sum", acc, 2)
    cells = lax.axis_size("comp") * chain * 2 * FACE * FACE
    return new[None, None], jnp.sqrt(total[0, 0] / cells)


def solution(mesh):
    wide = P("comp", "blk", None, None, None, None)
    cell = P("comp", "blk", None, None, None)
    return jax.shard_map(
        per_device,
        mesh=mesh,
        in_specs=(wide, wide, cell, cell, P()),
        out_specs=(wide, P()),
        check_vma=False,
    )
```

time: 350 us -> 77.9 us (0.22)
  blocking collectives: 201 us -> 0 us
  local copies, waits for them, and re-layouts: 68.5 us -> 2.21 us
  Pallas kernels: 0 us -> 61.4 us
  other arithmetic: 58.1 us -> 0.67 us
  between operations: 6.85 us -> 2.49 us
    pmin x1 -> x0, blocking collectives: 106 us -> none  [per_device(): smallest = lax.pmin(limit, ('comp', 'blk'))]
    psum x1 -> x0, blocking collectives: 95.4 us -> none  [per_device(): summed_terms = lax.psum(partial_value, ('comp', 'blk'))]
    pallas_call x0 -> x4, Pallas kernels: none -> 61.4 us  [the longest x2 42.1 us: reduce_all(): pl.pallas_call(functools.partial(reduce_kernel, op), out_shape=jax.ShapeD...]
    rev x8 -> x0, local copies, waits for them, and re-layouts: 33 us -> none  [the longest x2 10.8 us: restore(): jnp.flip(result, 3) * field_sign(count, third, layers.dtype)]
    concatenate x11 -> x1, other arithmetic: 20.3 us -> 0.6 us  [per_device(): flags = jnp.concatenate([mine, after, ends])]
    slice x13 -> x0, local copies, waits for them, and re-layouts: 16.3 us -> none  [the longest x2 5.84 us: assemble(): return jnp.pad(stacked, ((0, 0), (0, 0), (2, 2), (2, 2)), mode='edge')]
    select_n x12 -> x0, other arithmetic: 13.7 us -> none  [the longest x2 4.49 us: reorient(): jnp.where(flags[1] > 0, jnp.flip(layers, 2) * field_sign(count, second, l...]
    unnamed x54 -> x4, local copies, waits for them, and re-layouts: 12.3 us -> 1.16 us
  transfers between devices with their start and end apart: 2 -> 2, of which waited for: 1 -> 0; matrix products, arithmetic and copies ran while one was open for 2% -> 2% of each run, Pallas kernels for 0% -> 44%
where the time goes in v1:
time: 77.9 us; the launch traced here: 77.5 us
  Pallas kernels  61.4 us (79%)
  starting transfers between devices  10.7 us (14%)
  between operations  2.49 us (3%)
  local copies, waits for them, and re-layouts  2.21 us (3%)
    pallas_call x2, Pallas kernels, reduce_all(): pl.pallas_call(functools.partial(reduce_kernel, op), out_shape=jax.ShapeD...  42.1 us
    pallas_call x1, Pallas kernels, per_device(): pl.pallas_call(local_kernel, out_shape=(f32((6,) + plane), f32((3,) + pla...  10.9 us
    ppermute x1, starting transfers between devices, per_device(): above = lax.ppermute(state, 'blk', [(i + 1, i) for i in range(chain - 1)])  8.79 us
    pallas_call x1, Pallas kernels, per_device(): pl.pallas_call(chain_kernel, out_shape=(f32((6,) + plane), f32((8, FACE))...  8.36 us
    ppermute x1, starting transfers between devices, per_device(): below = lax.ppermute(state, 'blk', [(i, i + 1) for i in range(chain - 1)])  1.92 us
  transfers between devices with their start and end apart: 2, of which 0 were waited for; matrix products, arithmetic and copies ran while one was open for 2% of the time, Pallas kernels for 44%

profile of v1, /device:TPU:1, one launch (start us, length us, event | category | flops | bytes accessed | tf_op | source)
XLA Modules:
  0.0 77.5 jit_solution(11903540275337572575)
XLA Ops:
  0.6 8.8 %collective-permute-start.1 = (f32[6,2,128,128]{3,2,1,0:T(8,128)}, f32[6,2,128,128]{3,2,1,0:T(8,128)S(1)}, u32[]{:S(2)}, u32[]{:S(2)}) collective-permute-start(f32[6,2,128,128]{3,2,1,0:T(8,128)} %bitcast.8), channel_id=1, source_target_pairs={{1,0},{2,1},{3,2},{4,3},{5,4},{6,5},{7,6},{8,7},{9,8},{10,9},{11,1... | collective-permute-start | bytes 2359304 | tf_op jit(solution)/shard_map/ppermute | solution.py:361
  9.4 1.9 %collective-permute-start = (f32[6,2,128,128]{3,2,1,0:T(8,128)}, f32[6,2,128,128]{3,2,1,0:T(8,128)S(1)}, u32[]{:S(2)}, u32[]{:S(2)}) collective-permute-start(f32[6,2,128,128]{3,2,1,0:T(8,128)} %bitcast.9), channel_id=1, source_target_pairs={{0,1},{1,2},{2,3},{3,4},{4,5},{5,6},{6,7},{7,8},{8,9},{9,10},{10,1... | collective-permute-start | bytes 2359304 | tf_op jit(solution)/shard_map/ppermute | solution.py:360
  11.4 10.9 %local_flux.1 = (f32[6,2,128,128]{3,2,1,0:T(8,128)}, f32[3,2,128,128]{3,2,1,0:T(8,128)}, f32[8,128]{1,0:T(8,128)}) custom-call(f32[6,2,128,128]{3,2,1,0:T(8,128)} %bitcast.10, f32[2,128,128]{2,1,0:T(8,128)} %bitcast.13), custom_call_target="tpu_custom_call" | custom-call | flops 40000000 | bytes 3000000 | tf_op jit(solution)/shard_map/local_flux/pallas_call | solution.py:363
  22.2 23.2 %reduce_min.1.least = f32[1,1]{1,0:T(1,128)} custom-call(f32[8,128]{1,0:T(8,128)} %get-tuple-element.7.value), custom_call_target="tpu_custom_call" | custom-call | flops 1000 | bytes 1048576 | tf_op jit(solution)/shard_map/reduce_min/pallas_call | solution.py:334
  45.4 1.1 %dynamic-slice_reduce_fusion.1 = (s32[3]{0:T(128)S(1)}, s32[3]{0:T(128)S(1)}) fusion(s32[8,64,3]{1,0,2:T(8,128)} %param.9, s32[]{:T(128)S(6)} %select_n.18, s32[]{:T(128)S(6)} %select_n.20, s32[]{:T(128)S(6)} %select_n.22), kind=kLoop, calls=%fused_computation.2 | loop fusion | bytes 60 | tf_op jit(solution)/shard_map/jit(dynamic_index_in_dim)/dynamic_slice | solution.py:377
  46.5 0.1 add_convert_fusion
  46.6 0.6 pad_add_fusion.flags
  47.2 0.0 collective-permute-done.1.above
  47.2 0.0 copy-start
  47.2 0.0 collective-permute-done.below
  47.2 0.0 copy-start.1
  47.2 0.9 %copy-done = f32[6,2,128,128]{3,2,1,0:T(8,128)} copy-done((f32[6,2,128,128]{3,2,1,0:T(8,128)}, f32[6,2,128,128]{3,2,1,0:T(8,128)S(1)}, u32[]{:S(2)}) %copy-start) | copy-done | bytes 786456
  48.1 0.3 copy-done.1
  48.3 8.4 %chain_flux.1 = (f32[6,2,128,128]{3,2,1,0:T(8,128)}, f32[8,128]{1,0:T(8,128)}) custom-call(s32[8]{0:T(128)} %pad_add_fusion.flags, f32[1,1]{1,0:T(1,128)} %reduce_min.1.least, f32[6,2,128,128]{3,2,1,0:T(8,128)} %bitcast.11, f32[6,2,128,128]{3,2,1,0:T(8,128)} %bitcast.12, f32[2,128,128]{2,1,0:T(8,128)} %bitcast.14, f32[2,128,128]{2,1,0:T(8,128)} %bitcast.15, ...), custom_call_target="tpu_custom_call" | custom-call | flops 40000000 | bytes 5000000 | tf_op jit(solution)/shard_map/chain_flux/pallas_call | solution.py:382
  56.7 19.0 %reduce_sum.1 = f32[1,1]{1,0:T(1,128)} custom-call(f32[8,128]{1,0:T(8,128)} %get-tuple-element.11.value), custom_call_target="tpu_custom_call" | custom-call | flops 1000 | bytes 1048576 | tf_op jit(solution)/shard_map/reduce_sum/pallas_call | solution.py:334
Async XLA Ops:
  0.6 46.5 %collective-permute-start.1 = (f32[6,2,128,128]{3,2,1,0:T(8,128)}, f32[6,2,128,128]{3,2,1,0:T(8,128)S(1)}, u32[]{:S(2)}, u32[]{:S(2)}) collective-permute-start(f32[6,2,128,128]{3,2,1,0:T(8,128)} %bitcast.8), channel_id=1, source_target_pairs={{1,0},{2,1},{3,2},{4,3},{5,4},{6,5},{7,6},{8,7},{9,8},{10,9},{11,1... | collective-permute-start | bytes 2359304 | tf_op jit(solution)/shard_map/ppermute | solution.py:361
  9.4 37.7 %collective-permute-start = (f32[6,2,128,128]{3,2,1,0:T(8,128)}, f32[6,2,128,128]{3,2,1,0:T(8,128)S(1)}, u32[]{:S(2)}, u32[]{:S(2)}) collective-permute-start(f32[6,2,128,128]{3,2,1,0:T(8,128)} %bitcast.9), channel_id=1, source_target_pairs={{0,1},{1,2},{2,3},{3,4},{4,5},{5,6},{6,7},{7,8},{8,9},{9,10},{10,1... | collective-permute-start | bytes 2359304 | tf_op jit(solution)/shard_map/ppermute | solution.py:360
  47.2 0.9 %copy-start = (f32[6,2,128,128]{3,2,1,0:T(8,128)}, f32[6,2,128,128]{3,2,1,0:T(8,128)S(1)}, u32[]{:S(2)}) copy-start(f32[6,2,128,128]{3,2,1,0:T(8,128)S(1)} %collective-permute-done.1.above) | copy-start | bytes 2359300
  47.2 1.2 %copy-start.1 = (f32[6,2,128,128]{3,2,1,0:T(8,128)}, f32[6,2,128,128]{3,2,1,0:T(8,128)S(1)}, u32[]{:S(2)}) copy-start(f32[6,2,128,128]{3,2,1,0:T(8,128)S(1)} %collective-permute-done.below) | copy-start | bytes 2359300

commit v2 on v1

v2 whole, which is shorter than its diff:
```python
import functools

import jax
import jax.numpy as jnp
from jax import lax
from jax.experimental import pallas as pl
from jax.experimental.pallas import tpu as pltpu
from jax.sharding import PartitionSpec as P

GAMMA = 1.4
HEAT = 1.4 / (0.4 * 0.72)
CUBE = 7.1 * 7.1 * 7.1
MESH = pl.DeviceIdType.MESH
VMEM = pltpu.VMEM
FACE = 128
PAD = 8


def primitives(w):
    inv = 1.0 / w[0]
    u = [w[1] * inv, w[2] * inv, w[3] * inv]
    kinetic = 0.5 * (w[1] * u[0] + w[2] * u[1] + w[3] * u[2])
    p = 0.4 * (w[4] - kinetic)
    heat = p * inv
    cs = jnp.sqrt(GAMMA * heat)
    chi = w[5] * 20.0
    cubed = chi * chi * chi
    mu = w[5] * cubed / (cubed + CUBE)
    h = 0.5 * (u[0] * u[0] + u[1] * u[1] + u[2] * u[2]) + HEAT * heat
    return {"u": u, "p": p, "cs": cs, "mu": mu, "h": h, "nu": w[5] * inv}


def sensor(before, middle, after):
    twice = 2.0 * middle
    total = after + before
    return jnp.abs(total - twice) / (total + twice)


def face_flux(a, wm, w0, w1, w2, q0, q1, s0, s1, fields=range(6)):
    un0, un1 = q0["u"][a - 1], q1["u"][a - 1]
    half = 0.5 * ((jnp.abs(un0) + q0["cs"]) + (jnp.abs(un1) + q1["cs"]))
    e2 = 0.25 * jnp.maximum(s0, s1)
    e4 = jnp.maximum(0.0, 0.03125 - e2)
    b = half * e4
    c = half * e2 + 3.0 * b
    h0, h1 = 0.5 * un0, 0.5 * un1
    muf = 0.05 + 0.5 * (q0["mu"] + q1["mu"])
    out = []
    for f in fields:
        c0, c1 = w0[f], w1[f]
        if f == 4:
            c0, c1 = c0 + q0["p"], c1 + q1["p"]
        g = c0 * h0 + c1 * h1
        if f == a:
            g = g + 0.5 * (q0["p"] + q1["p"])
        g = g - c * (w1[f] - w0[f]) + b * (w2[f] - wm[f])
        if 1 <= f <= 3:
            g = g - muf * (q1["u"][f - 1] - q0["u"][f - 1])
        elif f == 4:
            g = g - muf * (q1["h"] - q0["h"])
        elif f == 5:
            g = g - (0.075 + 0.75 * (w0[5] + w1[5])) * (q1["nu"] - q0["nu"])
        out.append(g)
    return out


def edge_flux(a, w0, w1, q0, s0):
    un = q0["u"][a - 1]
    b = (jnp.abs(un) + q0["cs"]) * jnp.maximum(0.0, 0.03125 - 0.25 * s0)
    out = []
    for f in range(6):
        c0 = w0[f] + q0["p"] if f == 4 else w0[f]
        g = c0 * un
        if f == a:
            g = g + q0["p"]
        out.append(g + b * (w1[f] - w0[f]))
    return out


ROWS = 8
STEPS = FACE // ROWS
ORDER = ((2, 3), (0,), (1,), (4,), (5,))


def kernel(refs):
    comp, blk = lax.axis_index("comp"), lax.axis_index("blk")
    chain = lax.axis_size("blk")
    flags, state_hbm, volume_hbm, distance_hbm = refs["inputs"]
    change_hbm, least_out, total_out = refs["outputs"]
    state, volume, distance = refs["state"], refs["volume"], refs["distance"]
    wide, part, vort, change = refs["wide"], refs["part"], refs["vort"], refs["change"]
    ghost, slots = refs["ghost"], refs["slots"]
    halo = (refs["halo"][:6], refs["halo"][6:])
    load_sem, hsend, hrecv, rsend, rrecv = refs["sems"]

    low, high = blk % 8, blk // 8
    phases = (
        (low, lambda j: (comp, high * 8 + j)),
        (comp, lambda j: (j, blk)),
        (high, lambda j: (comp, j * 8 + low)),
    )
    has_below, has_above = blk > 0, blk < chain - 1
    below_id = (comp, jnp.maximum(blk - 1, 0))
    above_id = (comp, jnp.minimum(blk + 1, chain - 1))

    barrier = pltpu.get_barrier_semaphore()
    for has, device in ((has_below, below_id), (has_above, above_id)):

        @pl.when(has)
        def _():
            pl.semaphore_signal(barrier, inc=1, device_id=device, device_id_type=MESH)

    for me, device in phases:
        for step in range(1, 8):
            pl.semaphore_signal(
                barrier, inc=1, device_id=device((me + step) % 8), device_id_type=MESH
            )

    loads = [
        pltpu.make_async_copy(state_hbm, state, load_sem.at[0]),
        pltpu.make_async_copy(volume_hbm, volume, load_sem.at[1]),
        pltpu.make_async_copy(distance_hbm, distance, load_sem.at[2]),
    ]
    for copy in loads:
        copy.start()
    for copy in loads:
        copy.wait()

    def rows_of(k):
        return pl.ds(pl.multiple_of(k * ROWS, ROWS), ROWS)

    def fill(k, least):
        at = rows_of(k)
        to = pl.ds(pl.multiple_of(k * ROWS + PAD, ROWS), ROWS)
        for layer in range(2):
            w = [state[f, layer, at, :] for f in range(6)]
            q = primitives(w)
            u = q["u"]
            for f in range(6):
                wide[f, layer, to, :] = w[f]
            for i, x in enumerate(u + [q["p"], q["cs"], q["mu"], q["h"], q["nu"]]):
                wide[6 + i, layer, to, :] = x
            speed = (jnp.abs(u[0]) + q["cs"]) + (jnp.abs(u[1]) + q["cs"]) + (jnp.abs(u[2]) + q["cs"])
            least = jnp.minimum(least, volume[layer, at, :] / speed)
        return least

    limit = lax.fori_loop(0, STEPS, fill, jnp.full((ROWS, FACE), jnp.inf, jnp.float32))
    for layer in range(2):
        for i in range(14):
            first_row = wide[i, layer, PAD : PAD + 1, :]
            last_row = wide[i, layer, PAD + FACE - 1 : PAD + FACE, :]
            wide[i, layer, PAD - 2 : PAD - 1, :] = first_row
            wide[i, layer, PAD - 1 : PAD, :] = first_row
            wide[i, layer, PAD + FACE : PAD + FACE + 1, :] = last_row
            wide[i, layer, PAD + FACE + 1 : PAD + FACE + 2, :] = last_row

    pl.semaphore_wait(
        barrier, 21 + has_below.astype(jnp.int32) + has_above.astype(jnp.int32)
    )

    def exchange(kind, n, step):
        me, device = phases[n]
        return pltpu.make_async_remote_copy(
            src_ref=slots.at[kind, n, me],
            dst_ref=slots.at[kind, n, me],
            send_sem=rsend.at[kind, n, step],
            recv_sem=rrecv.at[kind, n, me],
            device_id=device((me + step) % 8),
            device_id_type=MESH,
        )

    def send(kind, n, value):
        slots[kind, n, pl.ds(phases[n][0], 1)] = value[None]
        for step in range(1, 8):
            exchange(kind, n, step).start()

    def receive(kind, n, op):
        me, device = phases[n]
        for step in range(1, 8):
            other = (me + step) % 8
            pltpu.make_async_remote_copy(
                src_ref=slots.at[kind, n, me],
                dst_ref=slots.at[kind, n, other],
                send_sem=rsend.at[kind, n, step],
                recv_sem=rrecv.at[kind, n, other],
                device_id=device(other),
                device_id_type=MESH,
            ).wait_recv()
        held = slots[kind, n, 0]
        for j in range(1, 8):
            held = op(held, slots[kind, n, j])
        for step in range(1, 8):
            exchange(kind, n, step).wait_send()
        return held

    send(0, 0, limit)

    sides = ((has_below, has_above, above_id), (has_above, has_below, below_id))

    def halo_copy(side, f):
        return pltpu.make_async_remote_copy(
            src_ref=state_hbm.at[f],
            dst_ref=halo[side][f].at[0],
            send_sem=hsend.at[side, f],
            recv_sem=hrecv.at[side, f],
            device_id=sides[side][2],
            device_id_type=MESH,
        )

    for fields in ORDER:
        for f in fields:
            for side in range(2):

                @pl.when(sides[side][1])
                def _():
                    halo_copy(side, f).start()

    lane = lax.broadcasted_iota(jnp.int32, (ROWS, FACE), 1)
    row = lax.broadcasted_iota(jnp.int32, (ROWS, FACE), 0)
    first, last, top = lane == 0, lane == FACE - 1, row == 0

    def after(x):
        return jnp.where(last, x, pltpu.roll(x, FACE - 1, 1))

    def before(x):
        return jnp.where(first, x, pltpu.roll(x, 1, 1))

    def local_flux(layer):
        def load(i, k, offset):
            return wide[i, layer, pl.ds(k * ROWS + PAD + offset, ROWS), :]

        def cell(k, offset):
            v = [load(6 + i, k, offset) for i in range(8)]
            return {"u": v[:3], "p": v[3], "cs": v[4], "mu": v[5], "h": v[6], "nu": v[7]}

        def states(k, offset):
            return [load(f, k, offset) for f in range(6)]

        def body(k, carry):
            w0, q0 = states(k, 0), cell(k, 0)
            w1, q1 = states(k, 1), cell(k, 1)
            pm, p2 = load(9, k, -1), load(9, k, 2)
            s0 = sensor(pm, q0["p"], q1["p"])
            s1 = sensor(q0["p"], q1["p"], p2)
            g = face_flux(2, states(k, -1), w0, w1, states(k, 2), q0, q1, s0, s1)
            turned = [pltpu.roll(x, 1, 0) for x in g]
            total = [x - jnp.where(top, c, y) for x, y, c in zip(g, turned, carry)]
            d2u0 = 0.5 * (q1["u"][0] - load(6, k, -1))
            d2u2 = 0.5 * (q1["u"][2] - load(8, k, -1))
            w1 = [after(x) for x in w0]
            w2 = [after(x) for x in w1]
            wm = [before(x) for x in w0]
            q1 = {n: after(q0[n]) for n in ("p", "cs", "mu", "h", "nu")}
            q1["u"] = [after(x) for x in q0["u"]]
            s0 = sensor(before(q0["p"]), q0["p"], q1["p"])
            g = face_flux(3, wm, w0, w1, w2, q0, q1, s0, after(s0))
            edge = edge_flux(3, w0, w1, q0, s0)
            total = [
                t + (x - jnp.where(first, e, pltpu.roll(x, 1, 1)))
                for t, x, e in zip(total, g, edge)
            ]
            d3u0 = 0.5 * (q1["u"][0] - before(q0["u"][0]))
            d3u1 = 0.5 * (q1["u"][1] - before(q0["u"][1]))
            at = rows_of(k)
            for f in range(6):
                part[f, layer, at, :] = total[f]
            vort[0, layer, at, :] = d2u2 - d3u1
            vort[1, layer, at, :] = d3u0
            vort[2, layer, at, :] = d2u0
            return tuple(turned)

        w0, q0 = states(0, 0), cell(0, 0)
        p1 = load(9, 0, 1)
        init = edge_flux(2, w0, states(0, 1), q0, sensor(load(9, 0, -1), q0["p"], p1))
        lax.fori_loop(0, STEPS, body, tuple(init))

    local_flux(0)
    send(0, 1, receive(0, 0, jnp.minimum))
    local_flux(1)
    send(0, 2, receive(0, 1, jnp.minimum))

    def one_if(condition):
        return jnp.where(condition, 1, 0)

    up = jnp.minimum(blk + 1, chain - 1)
    t, r2, r3 = [flags[i, comp, blk] * one_if(has_below) for i in range(3)]
    lower = (t, t * r3 + (1 - t) * r2, t * r2 + (1 - t) * r3)
    upper = tuple(flags[i, comp, up] * one_if(has_above) for i in range(3))

    for fields in ORDER:
        for side, (t, flip_rows, flip_lanes) in enumerate((lower, upper)):
            buf = halo[side]
            for f in fields:

                @pl.when(sides[side][0])
                def _():
                    halo_copy(side, f).wait_recv()

                @pl.when(jnp.logical_not(sides[side][0]))
                def _():
                    for layer in range(2):
                        buf[f][0, layer] = state[f, side]

            for f in fields:
                for layer in range(2):
                    buf[f][1, layer] = buf[{2: 3, 3: 2}.get(f, f)][0, layer].T
            turn, reverse_rows, reverse_lanes = [
                jnp.broadcast_to(x, (ROWS, FACE)) > 0 for x in (t, flip_rows, flip_lanes)
            ]
            signs = {
                2: 1.0 - 2.0 * flip_rows.astype(jnp.float32),
                3: 1.0 - 2.0 * flip_lanes.astype(jnp.float32),
            }

            def place(k, _):
                pair = (rows_of(k), rows_of(STEPS - 1 - k))
                for f in fields:
                    for layer in range(2):
                        x = [
                            jnp.where(turn, buf[f][1, layer, at, :], buf[f][0, layer, at, :])
                            for at in pair
                        ]
                        flipped = [jnp.take_along_axis(y, ROWS - 1 - row, axis=0) for y in x]
                        for i in range(2):
                            y = jnp.where(reverse_rows, flipped[1 - i], x[i])
                            z = jnp.take_along_axis(y, FACE - 1 - lane, axis=1)
                            y = jnp.where(reverse_lanes, z, y)
                            if f in signs:
                                y = y * signs[f]
                            ghost[side, f, layer, pair[i], :] = y
                return 0

            lax.fori_loop(0, STEPS // 2, place, 0)

    least = receive(0, 2, jnp.minimum)
    least_out[...] = jnp.min(least, axis=(0, 1), keepdims=True)

    def own(i, layer, k):
        return wide[i, layer, pl.ds(pl.multiple_of(k * ROWS + PAD, ROWS), ROWS), :]

    def density(k, total):
        at = rows_of(k)
        rho, p, un, cs = [], [], [], []
        for side, layer in ((0, 0), (0, 1), (None, 0), (None, 1), (1, 0), (1, 1)):
            if side is None:
                rho.append(own(0, layer, k))
                un.append(own(6, layer, k))
                p.append(own(9, layer, k))
                cs.append(own(10, layer, k))
            else:
                w = [ghost[side, f, layer, at, :] for f in range(5)]
                q = primitives(w + [w[0]])
                rho.append(w[0])
                un.append(q["u"][0])
                p.append(q["p"])
                cs.append(q["cs"])
        s = [None] + [sensor(p[i - 1], p[i], p[i + 1]) for i in range(1, 5)]
        g = []
        for i in range(1, 4):
            half = 0.5 * ((jnp.abs(un[i]) + cs[i]) + (jnp.abs(un[i + 1]) + cs[i + 1]))
            e2 = 0.25 * jnp.maximum(s[i], s[i + 1])
            b = half * jnp.maximum(0.0, 0.03125 - e2)
            c = half * e2 + 3.0 * b
            g.append(
                0.5 * (rho[i] * un[i] + rho[i + 1] * un[i + 1])
                - c * (rho[i + 1] - rho[i])
                + b * (rho[i + 2] - rho[i - 1])
            )
        for layer in range(2):
            z = (part[0, layer, at, :] + (g[layer + 1] - g[layer])) / volume[layer, at, :]
            change[0, layer, at, :] = z
            total = total + z * z
        return total

    total = lax.fori_loop(0, STEPS, density, jnp.zeros((ROWS, FACE), jnp.float32))
    send(1, 0, total)

    def rest(k, _):
        at = rows_of(k)
        w, q = [], []
        for side, layer in ((0, 0), (0, 1), (None, 0), (None, 1), (1, 0), (1, 1)):
            if side is None:
                w.append([own(f, layer, k) for f in range(6)])
                v = [own(6 + i, layer, k) for i in range(8)]
                q.append({"u": v[:3], "p": v[3], "cs": v[4], "mu": v[5], "h": v[6], "nu": v[7]})
            else:
                w.append([ghost[side, f, layer, at, :] for f in range(6)])
                q.append(primitives(w[-1]))
        s = [None] + [sensor(q[i - 1]["p"], q[i]["p"], q[i + 1]["p"]) for i in range(1, 5)]
        fields = range(1, 6)
        g = [
            face_flux(1, w[i - 1], w[i], w[i + 1], w[i + 2], q[i], q[i + 1], s[i], s[i + 1], fields)
            for i in range(1, 4)
        ]
        for layer in range(2):
            i = layer + 2
            vol = volume[layer, at, :]
            inv = 1.0 / vol
            d1u1 = 0.5 * (q[i + 1]["u"][1] - q[i - 1]["u"][1])
            d1u2 = 0.5 * (q[i + 1]["u"][2] - q[i - 1]["u"][2])
            w1 = vort[0, layer, at, :]
            w2 = vort[1, layer, at, :] - d1u2
            w3 = d1u1 - vort[2, layer, at, :]
            spin = jnp.sqrt(w1 * w1 + w2 * w2 + w3 * w3 + 1e-6)
            ratio = q[i]["nu"] / distance[layer, at, :]
            source = 0.1355 * spin * w[i][5] - 3.239 * w[i][0] * (ratio * ratio)
            for f in fields:
                r = part[f, layer, at, :] + (g[layer + 1][f - 1] - g[layer][f - 1])
                if f == 5:
                    r = r - vol * source
                change[f, layer, at, :] = r * inv
        return 0

    lax.fori_loop(0, 6, rest, 0)
    send(1, 1, receive(1, 0, jnp.add))
    lax.fori_loop(6, STEPS, rest, 0)
    store = pltpu.make_async_copy(change, change_hbm, load_sem.at[3])
    store.start()
    send(1, 2, receive(1, 1, jnp.add))
    for side in range(2):
        for f in range(6):

            @pl.when(sides[side][1])
            def _():
                halo_copy(side, f).wait_send()

    total_out[...] = jnp.sum(receive(1, 2, jnp.add), axis=(0, 1), keepdims=True)
    store.wait()


def entry(*args):
    names = ("state", "volume", "distance", "wide", "part", "vort", "change", "ghost", "slots")
    refs = {"inputs": args[:4], "outputs": args[4:7]}
    refs.update(zip(names, args[7:16]))
    refs["halo"] = args[16:28]
    refs["sems"] = args[28:]
    kernel(refs)


def per_device(base_state, section_state, volume, distance, orientation):
    f32 = functools.partial(jax.ShapeDtypeStruct, dtype=jnp.float32)
    scratch = functools.partial(VMEM, dtype=jnp.float32)
    hbm = pl.BlockSpec(memory_space=pl.ANY)
    vm = pl.BlockSpec(memory_space=VMEM)
    plane = (2, FACE, FACE)
    dma = pltpu.SemaphoreType.DMA
    change, least, total = pl.pallas_call(
        entry,
        out_shape=(f32((6,) + plane), f32((1, 1)), f32((1, 1))),
        in_specs=[pl.BlockSpec(memory_space=pltpu.SMEM), hbm, hbm, hbm],
        out_specs=(hbm, vm, vm),
        scratch_shapes=[
            scratch((6,) + plane),
            scratch(plane),
            scratch(plane),
            scratch((14, 2, FACE + 2 * PAD, FACE)),
            scratch((6,) + plane),
            scratch((3,) + plane),
            scratch((6,) + plane),
            scratch((2, 6) + plane),
            scratch((2, 3, 8, 8, FACE)),
        ]
        + [scratch((2,) + plane)] * 12
        + [dma((4,)), dma((2, 6)), dma((2, 6)), dma((2, 3, 8)), dma((2, 3, 8))],
        compiler_params=pltpu.CompilerParams(collective_id=1, has_side_effects=True),
        cost_estimate=pl.CostEstimate(
            flops=80_000_000, bytes_accessed=4_000_000, transcendentals=800_000
        ),
        name="section",
    )(jnp.transpose(orientation, (2, 0, 1)), section_state[0, 0], volume[0, 0], distance[0, 0])
    new = base_state[0, 0] - least[0, 0] * change
    cells = lax.axis_size("comp") * lax.axis_size("blk") * 2 * FACE * FACE
    return new[None, None], jnp.sqrt(total[0, 0] / cells)


def solution(mesh):
    wide = P("comp", "blk", None, None, None, None)
    cell = P("comp", "blk", None, None, None)
    return jax.shard_map(
        per_device,
        mesh=mesh,
        in_specs=(wide, wide, cell, cell, P()),
        out_specs=(wide, P()),
        check_vma=False,
    )
```

time: 77.9 us -> 57.6 us (0.74)
  the two profiles are of different devices: /device:TPU:1 before, /device:TPU:4 now
where the time goes in v2:
time: 57.6 us; the launch traced here: 57.3 us
  Pallas kernels  52.2 us (91%)
  other arithmetic  2.73 us (5%)
  between operations  2.45 us (4%)
    pallas_call x1, Pallas kernels, per_device(): pl.pallas_call(entry, out_shape=(f32((6,) + plane), f32((1, 1)), f32((1,...  52.2 us
    broadcast_in_dim x1, other arithmetic, per_device(): return (new[None, None], jnp.sqrt(total[0, 0] / cells))  2.73 us

profile of v2, /device:TPU:4, one launch (start us, length us, event | category | flops | bytes accessed | tf_op | source)
XLA Modules:
  0.0 57.3 jit_solution(3482390493307280472)
XLA Ops:
  0.6 0.0 copy-start
  0.6 52.2 %section.1 = (f32[6,2,128,128]{3,2,1,0:T(8,128)}, f32[1,1]{1,0:T(1,128)}, f32[1,1]{1,0:T(1,128)}) custom-call(s32[3,8,64]{2,1,0:T(8,128)} %bitcast.15, f32[6,2,128,128]{3,2,1,0:T(8,128)} %bitcast.12, f32[2,128,128]{2,1,0:T(8,128)} %bitcast.13, f32[2,128,128]{2,1,0:T(8,128)} %bitcast.14), custom_call_target="tpu_custom_call" | custom-call | flops 80000000 | bytes 4000000 | tf_op jit(solution)/shard_map/section/pallas_call | solution.py:447
  53.5 0.0 copy-done
  53.5 2.7 %fusion = f32[1,1,6,2,128,128]{5,4,3,2,1,0:T(8,128)} fusion(f32[1,1,6,2,128,128]{5,4,3,2,1,0:T(8,128)S(1)} %copy-done, f32[6,2,128,128]{3,2,1,0:T(8,128)} %get-tuple-element.6, f32[]{:T(128)} %bitcast.5), kind=kLoop, calls=%fused_computation.1 | loop fusion | flops 393216 | bytes 2359300 | tf_op jit(solution)/shard_map/broadcast_in_dim | solution.py:473
Async XLA Ops:
  0.6 52.8 %copy-start = (f32[1,1,6,2,128,128]{5,4,3,2,1,0:T(8,128)S(1)}, f32[1,1,6,2,128,128]{5,4,3,2,1,0:T(8,128)}, u32[]{:S(2)}) copy-start(f32[1,1,6,2,128,128]{5,4,3,2,1,0:T(8,128)} %param.5) | copy-start | bytes 2359300

commit v3 on v2

--- a/solution.py
+++ b/solution.py
@@ -64,11 +64,11 @@
     return out
 
 
-def edge_flux(a, w0, w1, q0, s0):
+def edge_flux(a, w0, w1, q0, s0, fields=range(6)):
     un = q0["u"][a - 1]
     b = (jnp.abs(un) + q0["cs"]) * jnp.maximum(0.0, 0.03125 - 0.25 * s0)
     out = []
-    for f in range(6):
+    for f in fields:
         c0 = w0[f] + q0["p"] if f == 4 else w0[f]
         g = c0 * un
         if f == a:
@@ -85,8 +85,9 @@
 def kernel(refs):
     comp, blk = lax.axis_index("comp"), lax.axis_index("blk")
     chain = lax.axis_size("blk")
-    flags, state_hbm, volume_hbm, distance_hbm = refs["inputs"]
-    change_hbm, least_out, total_out = refs["outputs"]
+    flags_hbm, state_hbm, volume_hbm, distance_hbm, base_hbm = refs["inputs"]
+    new_hbm, total_out = refs["outputs"]
+    flags, base = refs["flags"], refs["base"]
     state, volume, distance = refs["state"], refs["volume"], refs["distance"]
     wide, part, vort, change = refs["wide"], refs["part"], refs["vort"], refs["change"]
     ghost, slots = refs["ghost"], refs["slots"]
@@ -103,6 +104,21 @@
     below_id = (comp, jnp.maximum(blk - 1, 0))
     above_id = (comp, jnp.minimum(blk + 1, chain - 1))
 
+    loads = [
+        pltpu.make_async_copy(source, target, load_sem.at[i])
+        for i, (source, target) in enumerate(
+            (
+                (state_hbm, state),
+                (volume_hbm, volume),
+                (flags_hbm, flags),
+                (distance_hbm, distance),
+                (base_hbm, base),
+            )
+        )
+    ]
+    for copy in loads:
+        copy.start()
+
     barrier = pltpu.get_barrier_semaphore()
     for has, device in ((has_below, below_id), (has_above, above_id)):
 
@@ -116,20 +132,13 @@
                 barrier, inc=1, device_id=device((me + step) % 8), device_id_type=MESH
             )
 
-    loads = [
-        pltpu.make_async_copy(state_hbm, state, load_sem.at[0]),
-        pltpu.make_async_copy(volume_hbm, volume, load_sem.at[1]),
-        pltpu.make_async_copy(distance_hbm, distance, load_sem.at[2]),
-    ]
-    for copy in loads:
-        copy.start()
-    for copy in loads:
-        copy.wait()
-
     def rows_of(k):
         return pl.ds(pl.multiple_of(k * ROWS, ROWS), ROWS)
 
-    def fill(k, least):
+    loads[0].wait()
+    loads[1].wait()
+
+    def fill_rows(k, least):
         at = rows_of(k)
         to = pl.ds(pl.multiple_of(k * ROWS + PAD, ROWS), ROWS)
         for layer in range(2):
@@ -144,7 +153,10 @@
             least = jnp.minimum(least, volume[layer, at, :] / speed)
         return least
 
-    limit = lax.fori_loop(0, STEPS, fill, jnp.full((ROWS, FACE), jnp.inf, jnp.float32))
+    def fill(k, least):
+        return fill_rows(2 * k + 1, fill_rows(2 * k, least))
+
+    limit = lax.fori_loop(0, STEPS // 2, fill, jnp.full((ROWS, FACE), jnp.inf, jnp.float32))
     for layer in range(2):
         for i in range(14):
             first_row = wide[i, layer, PAD : PAD + 1, :]
@@ -225,7 +237,7 @@
     def before(x):
         return jnp.where(first, x, pltpu.roll(x, 1, 1))
 
-    def local_flux(layer):
+    def local_flux(layer, fields, vorticity, low, high, carry=None):
         def load(i, k, offset):
             return wide[i, layer, pl.ds(k * ROWS + PAD + offset, ROWS), :]
 
@@ -242,54 +254,62 @@
             pm, p2 = load(9, k, -1), load(9, k, 2)
             s0 = sensor(pm, q0["p"], q1["p"])
             s1 = sensor(q0["p"], q1["p"], p2)
-            g = face_flux(2, states(k, -1), w0, w1, states(k, 2), q0, q1, s0, s1)
+            g = face_flux(2, states(k, -1), w0, w1, states(k, 2), q0, q1, s0, s1, fields)
             turned = [pltpu.roll(x, 1, 0) for x in g]
             total = [x - jnp.where(top, c, y) for x, y, c in zip(g, turned, carry)]
-            d2u0 = 0.5 * (q1["u"][0] - load(6, k, -1))
-            d2u2 = 0.5 * (q1["u"][2] - load(8, k, -1))
             w1 = [after(x) for x in w0]
             w2 = [after(x) for x in w1]
             wm = [before(x) for x in w0]
             q1 = {n: after(q0[n]) for n in ("p", "cs", "mu", "h", "nu")}
             q1["u"] = [after(x) for x in q0["u"]]
             s0 = sensor(before(q0["p"]), q0["p"], q1["p"])
-            g = face_flux(3, wm, w0, w1, w2, q0, q1, s0, after(s0))
-            edge = edge_flux(3, w0, w1, q0, s0)
+            g = face_flux(3, wm, w0, w1, w2, q0, q1, s0, after(s0), fields)
+            edge = edge_flux(3, w0, w1, q0, s0, fields)
             total = [
                 t + (x - jnp.where(first, e, pltpu.roll(x, 1, 1)))
                 for t, x, e in zip(total, g, edge)
             ]
-            d3u0 = 0.5 * (q1["u"][0] - before(q0["u"][0]))
-            d3u1 = 0.5 * (q1["u"][1] - before(q0["u"][1]))
             at = rows_of(k)
-            for f in range(6):
-                part[f, layer, at, :] = total[f]
-            vort[0, layer, at, :] = d2u2 - d3u1
-            vort[1, layer, at, :] = d3u0
-            vort[2, layer, at, :] = d2u0
+            for f, x in zip(fields, total):
+                part[f, layer, at, :] = x
+            if vorticity:
+                u1 = [load(6, k, 1), load(8, k, 1)]
+                d2u0 = 0.5 * (u1[0] - load(6, k, -1))
+                d2u2 = 0.5 * (u1[1] - load(8, k, -1))
+                d3u0 = 0.5 * (q1["u"][0] - before(q0["u"][0]))
+                d3u1 = 0.5 * (q1["u"][1] - before(q0["u"][1]))
+                vort[0, layer, at, :] = d2u2 - d3u1
+                vort[1, layer, at, :] = d3u0
+                vort[2, layer, at, :] = d2u0
             return tuple(turned)
 
-        w0, q0 = states(0, 0), cell(0, 0)
-        p1 = load(9, 0, 1)
-        init = edge_flux(2, w0, states(0, 1), q0, sensor(load(9, 0, -1), q0["p"], p1))
-        lax.fori_loop(0, STEPS, body, tuple(init))
-
-    local_flux(0)
+        if carry is None:
+            w0, q0 = states(0, 0), cell(0, 0)
+            s0 = sensor(load(9, 0, -1), q0["p"], load(9, 0, 1))
+            carry = edge_flux(2, w0, states(0, 1), q0, s0, fields)
+        return lax.fori_loop(low, high, body, tuple(carry))
+
+    for layer in range(2):
+        local_flux(layer, (0,), False, 0, STEPS)
     send(0, 1, receive(0, 0, jnp.minimum))
-    local_flux(1)
-    send(0, 2, receive(0, 1, jnp.minimum))
 
     def one_if(condition):
         return jnp.where(condition, 1, 0)
 
+    loads[2].wait()
     up = jnp.minimum(blk + 1, chain - 1)
     t, r2, r3 = [flags[i, comp, blk] * one_if(has_below) for i in range(3)]
     lower = (t, t * r3 + (1 - t) * r2, t * r2 + (1 - t) * r3)
     upper = tuple(flags[i, comp, up] * one_if(has_above) for i in range(3))
 
-    for fields in ORDER:
-        for side, (t, flip_rows, flip_lanes) in enumerate((lower, upper)):
-            buf = halo[side]
+    turns = []
+    for t, flip_rows, flip_lanes in (lower, upper):
+        masks = [jnp.broadcast_to(x, (ROWS, FACE)) > 0 for x in (t, flip_rows, flip_lanes)]
+        signs = [1.0 - 2.0 * x.astype(jnp.float32) for x in (flip_rows, flip_lanes)]
+        turns.append((masks, signs))
+
+    def arrive(fields):
+        for side in range(2):
             for f in fields:
 
                 @pl.when(sides[side][0])
@@ -299,25 +319,23 @@
                 @pl.when(jnp.logical_not(sides[side][0]))
                 def _():
                     for layer in range(2):
-                        buf[f][0, layer] = state[f, side]
-
+                        halo[side][f][0, layer] = state[f, side]
+
+        for side in range(2):
             for f in fields:
                 for layer in range(2):
-                    buf[f][1, layer] = buf[{2: 3, 3: 2}.get(f, f)][0, layer].T
-            turn, reverse_rows, reverse_lanes = [
-                jnp.broadcast_to(x, (ROWS, FACE)) > 0 for x in (t, flip_rows, flip_lanes)
-            ]
-            signs = {
-                2: 1.0 - 2.0 * flip_rows.astype(jnp.float32),
-                3: 1.0 - 2.0 * flip_lanes.astype(jnp.float32),
-            }
-
-            def place(k, _):
-                pair = (rows_of(k), rows_of(STEPS - 1 - k))
+                    source = halo[side][{2: 3, 3: 2}.get(f, f)]
+                    halo[side][f][1, layer] = source[0, layer].T
+
+        def place(k, _):
+            pair = (rows_of(k), rows_of(STEPS - 1 - k))
+            for side in range(2):
+                (turn, reverse_rows, reverse_lanes), signs = turns[side]
                 for f in fields:
+                    buf = halo[side][f]
                     for layer in range(2):
                         x = [
-                            jnp.where(turn, buf[f][1, layer, at, :], buf[f][0, layer, at, :])
+                            jnp.where(turn, buf[1, layer, at, :], buf[0, layer, at, :])
                             for at in pair
                         ]
                         flipped = [jnp.take_along_axis(y, ROWS - 1 - row, axis=0) for y in x]
@@ -325,20 +343,23 @@
                             y = jnp.where(reverse_rows, flipped[1 - i], x[i])
                             z = jnp.take_along_axis(y, FACE - 1 - lane, axis=1)
                             y = jnp.where(reverse_lanes, z, y)
-                            if f in signs:
-                                y = y * signs[f]
+                            if f in (2, 3):
+                                y = y * signs[f - 2]
                             ghost[side, f, layer, pair[i], :] = y
-                return 0
-
-            lax.fori_loop(0, STEPS // 2, place, 0)
-
-    least = receive(0, 2, jnp.minimum)
-    least_out[...] = jnp.min(least, axis=(0, 1), keepdims=True)
+            return 0
+
+        lax.fori_loop(0, STEPS // 2, place, 0)
+
+    arrive(ORDER[0])
+    arrive(ORDER[1])
+    send(0, 2, receive(0, 1, jnp.minimum))
+    for fields in ORDER[2:]:
+        arrive(fields)
 
     def own(i, layer, k):
         return wide[i, layer, pl.ds(pl.multiple_of(k * ROWS + PAD, ROWS), ROWS), :]
 
-    def density(k, total):
+    def density_rows(k, total):
         at = rows_of(k)
         rho, p, un, cs = [], [], [], []
         for side, layer in ((0, 0), (0, 1), (None, 0), (None, 1), (1, 0), (1, 1)):
@@ -372,7 +393,10 @@
             total = total + z * z
         return total
 
-    total = lax.fori_loop(0, STEPS, density, jnp.zeros((ROWS, FACE), jnp.float32))
+    def density(k, total):
+        return density_rows(2 * k + 1, density_rows(2 * k, total))
+
+    total = lax.fori_loop(0, STEPS // 2, density, jnp.zeros((ROWS, FACE), jnp.float32))
     send(1, 0, total)
 
     def rest(k, _):
@@ -408,15 +432,23 @@
                 r = part[f, layer, at, :] + (g[layer + 1][f - 1] - g[layer][f - 1])
                 if f == 5:
                     r = r - vol * source
-                change[f, layer, at, :] = r * inv
+                change[f, layer, at, :] = base[f, layer, at, :] - least * (r * inv)
+            change[0, layer, at, :] = base[0, layer, at, :] - least * change[0, layer, at, :]
         return 0
 
-    lax.fori_loop(0, 6, rest, 0)
+    others = (1, 2, 3, 4, 5)
+    held = local_flux(0, others, True, 0, 8)
+    least = receive(0, 2, jnp.minimum)
+    least = jnp.broadcast_to(jnp.min(least, axis=(0, 1), keepdims=True), (ROWS, FACE))
     send(1, 1, receive(1, 0, jnp.add))
-    lax.fori_loop(6, STEPS, rest, 0)
-    store = pltpu.make_async_copy(change, change_hbm, load_sem.at[3])
+    local_flux(0, others, True, 8, STEPS, held)
+    local_flux(1, others, True, 0, STEPS)
+    send(1, 2, receive(1, 1, jnp.add))
+    loads[3].wait()
+    loads[4].wait()
+    lax.fori_loop(0, STEPS, rest, 0)
+    store = pltpu.make_async_copy(change, new_hbm, load_sem.at[5])
     store.start()
-    send(1, 2, receive(1, 1, jnp.add))
     for side in range(2):
         for f in range(6):
 
@@ -429,11 +461,12 @@
 
 
 def entry(*args):
-    names = ("state", "volume", "distance", "wide", "part", "vort", "change", "ghost", "slots")
-    refs = {"inputs": args[:4], "outputs": args[4:7]}
-    refs.update(zip(names, args[7:16]))
-    refs["halo"] = args[16:28]
-    refs["sems"] = args[28:]
+    names = ("flags", "state", "base", "volume", "distance", "wide", "part", "vort")
+    names = names + ("change", "ghost", "slots")
+    refs = {"inputs": args[:5], "outputs": args[5:7]}
+    refs.update(zip(names, args[7:18]))
+    refs["halo"] = args[18:30]
+    refs["sems"] = args[30:]
     kernel(refs)
 
 
@@ -441,15 +474,17 @@
     f32 = functools.partial(jax.ShapeDtypeStruct, dtype=jnp.float32)
     scratch = functools.partial(VMEM, dtype=jnp.float32)
     hbm = pl.BlockSpec(memory_space=pl.ANY)
-    vm = pl.BlockSpec(memory_space=VMEM)
     plane = (2, FACE, FACE)
     dma = pltpu.SemaphoreType.DMA
-    change, least, total = pl.pallas_call(
+    flags = jnp.transpose(orientation, (2, 0, 1))
+    new, total = pl.pallas_call(
         entry,
-        out_shape=(f32((6,) + plane), f32((1, 1)), f32((1, 1))),
-        in_specs=[pl.BlockSpec(memory_space=pltpu.SMEM), hbm, hbm, hbm],
-        out_specs=(hbm, vm, vm),
+        out_shape=(f32((6,) + plane), f32((1, 1))),
+        in_specs=[hbm] * 5,
+        out_specs=(hbm, pl.BlockSpec(memory_space=VMEM)),
         scratch_shapes=[
+            pltpu.SMEM(flags.shape, jnp.int32),
+            scratch((6,) + plane),
             scratch((6,) + plane),
             scratch(plane),
             scratch(plane),
@@ -461,14 +496,13 @@
             scratch((2, 3, 8, 8, FACE)),
         ]
         + [scratch((2,) + plane)] * 12
-        + [dma((4,)), dma((2, 6)), dma((2, 6)), dma((2, 3, 8)), dma((2, 3, 8))],
+        + [dma((6,)), dma((2, 6)), dma((2, 6)), dma((2, 3, 8)), dma((2, 3, 8))],
         compiler_params=pltpu.CompilerParams(collective_id=1, has_side_effects=True),
         cost_estimate=pl.CostEstimate(
             flops=80_000_000, bytes_accessed=4_000_000, transcendentals=800_000
         ),
         name="section",
-    )(jnp.transpose(orientation, (2, 0, 1)), section_state[0, 0], volume[0, 0], distance[0, 0])
-    new = base_state[0, 0] - least[0, 0] * change
+    )(flags, section_state[0, 0], volume[0, 0], distance[0, 0], base_state[0, 0])
     cells = lax.axis_size("comp") * lax.axis_size("blk") * 2 * FACE * FACE
     return new[None, None], jnp.sqrt(total[0, 0] / cells)
 

time: 57.6 us -> 50.5 us (0.88)
  the two profiles are of different devices: /device:TPU:4 before, /device:TPU:1 now
where the time goes in v3:
time: 50.5 us; the launch traced here: 50.2 us
  Pallas kernels  45.7 us (90%)
  between operations  2.36 us (5%)
  local copies, waits for them, and re-layouts  2.06 us (4%)
    pallas_call x1, Pallas kernels, per_device(): pl.pallas_call(entry, out_shape=(f32((6,) + plane), f32((1, 1))), in_spec...  45.7 us
    unnamed x1, local copies, waits for them, and re-layouts  2.06 us

profile of v3, /device:TPU:1, one launch (start us, length us, event | category | flops | bytes accessed | tf_op | source)
XLA Modules:
  0.0 50.2 jit_solution(7855544590924276298)
XLA Ops:
  0.6 45.7 %section.1 = (f32[6,2,128,128]{3,2,1,0:T(8,128)}, f32[1,1]{1,0:T(1,128)}) custom-call(s32[3,8,64]{2,1,0:T(8,128)} %bitcast.12, f32[6,2,128,128]{3,2,1,0:T(8,128)} %bitcast.7, f32[2,128,128]{2,1,0:T(8,128)} %bitcast.10, f32[2,128,128]{2,1,0:T(8,128)} %bitcast.11, f32[6,2,128,128]{3,2,1,0:T(8,128)} %bitcast.8), custom_call_target="tpu_custom_call" | custom-call | flops 80000000 | bytes 4000000 | tf_op jit(solution)/shard_map/section/pallas_call | solution.py:480
  47.0 2.1 %copy.8 = f32[1,1,6,2,128,128]{5,4,3,2,1,0:T(8,128)} copy(f32[1,1,6,2,128,128]{5,4,3,2,1,0:T(8,128)} %bitcast.9) | data formatting | bytes 1572864

commit v4 on v3

--- a/solution.py
+++ b/solution.py
@@ -86,10 +86,10 @@
     comp, blk = lax.axis_index("comp"), lax.axis_index("blk")
     chain = lax.axis_size("blk")
     flags_hbm, state_hbm, volume_hbm, distance_hbm, base_hbm = refs["inputs"]
-    new_hbm, total_out = refs["outputs"]
+    change, total_out = refs["outputs"]
     flags, base = refs["flags"], refs["base"]
     state, volume, distance = refs["state"], refs["volume"], refs["distance"]
-    wide, part, vort, change = refs["wide"], refs["part"], refs["vort"], refs["change"]
+    wide, part, vort = refs["wide"], refs["part"], refs["vort"]
     ghost, slots = refs["ghost"], refs["slots"]
     halo = (refs["halo"][:6], refs["halo"][6:])
     load_sem, hsend, hrecv, rsend, rrecv = refs["sems"]
@@ -134,37 +134,6 @@
 
     def rows_of(k):
         return pl.ds(pl.multiple_of(k * ROWS, ROWS), ROWS)
-
-    loads[0].wait()
-    loads[1].wait()
-
-    def fill_rows(k, least):
-        at = rows_of(k)
-        to = pl.ds(pl.multiple_of(k * ROWS + PAD, ROWS), ROWS)
-        for layer in range(2):
-            w = [state[f, layer, at, :] for f in range(6)]
-            q = primitives(w)
-            u = q["u"]
-            for f in range(6):
-                wide[f, layer, to, :] = w[f]
-            for i, x in enumerate(u + [q["p"], q["cs"], q["mu"], q["h"], q["nu"]]):
-                wide[6 + i, layer, to, :] = x
-            speed = (jnp.abs(u[0]) + q["cs"]) + (jnp.abs(u[1]) + q["cs"]) + (jnp.abs(u[2]) + q["cs"])
-            least = jnp.minimum(least, volume[layer, at, :] / speed)
-        return least
-
-    def fill(k, least):
-        return fill_rows(2 * k + 1, fill_rows(2 * k, least))
-
-    limit = lax.fori_loop(0, STEPS // 2, fill, jnp.full((ROWS, FACE), jnp.inf, jnp.float32))
-    for layer in range(2):
-        for i in range(14):
-            first_row = wide[i, layer, PAD : PAD + 1, :]
-            last_row = wide[i, layer, PAD + FACE - 1 : PAD + FACE, :]
-            wide[i, layer, PAD - 2 : PAD - 1, :] = first_row
-            wide[i, layer, PAD - 1 : PAD, :] = first_row
-            wide[i, layer, PAD + FACE : PAD + FACE + 1, :] = last_row
-            wide[i, layer, PAD + FACE + 1 : PAD + FACE + 2, :] = last_row
 
     pl.semaphore_wait(
         barrier, 21 + has_below.astype(jnp.int32) + has_above.astype(jnp.int32)
@@ -205,8 +174,6 @@
             exchange(kind, n, step).wait_send()
         return held
 
-    send(0, 0, limit)
-
     sides = ((has_below, has_above, above_id), (has_above, has_below, below_id))
 
     def halo_copy(side, f):
@@ -219,13 +186,49 @@
             device_id_type=MESH,
         )
 
-    for fields in ORDER:
+    def send_halo(fields):
         for f in fields:
             for side in range(2):
 
                 @pl.when(sides[side][1])
                 def _():
                     halo_copy(side, f).start()
+
+    send_halo(ORDER[0])
+    loads[0].wait()
+    loads[1].wait()
+
+    def fill_rows(k, least):
+        at = rows_of(k)
+        to = pl.ds(pl.multiple_of(k * ROWS + PAD, ROWS), ROWS)
+        for layer in range(2):
+            w = [state[f, layer, at, :] for f in range(6)]
+            q = primitives(w)
+            u = q["u"]
+            for f in range(6):
+                wide[f, layer, to, :] = w[f]
+            for i, x in enumerate(u + [q["p"], q["cs"], q["mu"], q["h"], q["nu"]]):
+                wide[6 + i, layer, to, :] = x
+            speed = (jnp.abs(u[0]) + q["cs"]) + (jnp.abs(u[1]) + q["cs"]) + (jnp.abs(u[2]) + q["cs"])
+            least = jnp.minimum(least, volume[layer, at, :] / speed)
+        return least
+
+    def fill(k, least):
+        return fill_rows(2 * k + 1, fill_rows(2 * k, least))
+
+    limit = lax.fori_loop(0, STEPS // 2, fill, jnp.full((ROWS, FACE), jnp.inf, jnp.float32))
+    for layer in range(2):
+        for i in range(14):
+            first_row = wide[i, layer, PAD : PAD + 1, :]
+            last_row = wide[i, layer, PAD + FACE - 1 : PAD + FACE, :]
+            wide[i, layer, PAD - 2 : PAD - 1, :] = first_row
+            wide[i, layer, PAD - 1 : PAD, :] = first_row
+            wide[i, layer, PAD + FACE : PAD + FACE + 1, :] = last_row
+            wide[i, layer, PAD + FACE + 1 : PAD + FACE + 2, :] = last_row
+
+    send(0, 0, limit)
+    for fields in ORDER[1:]:
+        send_halo(fields)
 
     lane = lax.broadcasted_iota(jnp.int32, (ROWS, FACE), 1)
     row = lax.broadcasted_iota(jnp.int32, (ROWS, FACE), 0)
@@ -291,7 +294,6 @@
 
     for layer in range(2):
         local_flux(layer, (0,), False, 0, STEPS)
-    send(0, 1, receive(0, 0, jnp.minimum))
 
     def one_if(condition):
         return jnp.where(condition, 1, 0)
@@ -352,9 +354,9 @@
 
     arrive(ORDER[0])
     arrive(ORDER[1])
-    send(0, 2, receive(0, 1, jnp.minimum))
-    for fields in ORDER[2:]:
-        arrive(fields)
+    send(0, 1, receive(0, 0, jnp.minimum))
+    arrive(ORDER[2])
+    arrive(ORDER[3])
 
     def own(i, layer, k):
         return wide[i, layer, pl.ds(pl.multiple_of(k * ROWS + PAD, ROWS), ROWS), :]
@@ -398,6 +400,8 @@
 
     total = lax.fori_loop(0, STEPS // 2, density, jnp.zeros((ROWS, FACE), jnp.float32))
     send(1, 0, total)
+    send(0, 2, receive(0, 1, jnp.minimum))
+    arrive(ORDER[4])
 
     def rest(k, _):
         at = rows_of(k)
@@ -437,18 +441,16 @@
         return 0
 
     others = (1, 2, 3, 4, 5)
-    held = local_flux(0, others, True, 0, 8)
+    held = local_flux(0, others, True, 0, 4)
+    send(1, 1, receive(1, 0, jnp.add))
+    local_flux(0, others, True, 4, STEPS, held)
+    local_flux(1, others, True, 0, STEPS)
+    send(1, 2, receive(1, 1, jnp.add))
     least = receive(0, 2, jnp.minimum)
     least = jnp.broadcast_to(jnp.min(least, axis=(0, 1), keepdims=True), (ROWS, FACE))
-    send(1, 1, receive(1, 0, jnp.add))
-    local_flux(0, others, True, 8, STEPS, held)
-    local_flux(1, others, True, 0, STEPS)
-    send(1, 2, receive(1, 1, jnp.add))
     loads[3].wait()
     loads[4].wait()
     lax.fori_loop(0, STEPS, rest, 0)
-    store = pltpu.make_async_copy(change, new_hbm, load_sem.at[5])
-    store.start()
     for side in range(2):
         for f in range(6):
 
@@ -456,17 +458,18 @@
             def _():
                 halo_copy(side, f).wait_send()
 
-    total_out[...] = jnp.sum(receive(1, 2, jnp.add), axis=(0, 1), keepdims=True)
-    store.wait()
+    cells = lax.axis_size("comp") * chain * 2 * FACE * FACE
+    norm = jnp.sum(receive(1, 2, jnp.add), axis=(0, 1), keepdims=True)
+    total_out[...] = jnp.sqrt(norm / cells)
 
 
 def entry(*args):
     names = ("flags", "state", "base", "volume", "distance", "wide", "part", "vort")
-    names = names + ("change", "ghost", "slots")
+    names = names + ("ghost", "slots")
     refs = {"inputs": args[:5], "outputs": args[5:7]}
-    refs.update(zip(names, args[7:18]))
-    refs["halo"] = args[18:30]
-    refs["sems"] = args[30:]
+    refs.update(zip(names, args[7:17]))
+    refs["halo"] = args[17:29]
+    refs["sems"] = args[29:]
     kernel(refs)
 
 
@@ -479,9 +482,9 @@
     flags = jnp.transpose(orientation, (2, 0, 1))
     new, total = pl.pallas_call(
         entry,
-        out_shape=(f32((6,) + plane), f32((1, 1))),
+        out_shape=(scratch((6,) + plane), f32((1, 1))),
         in_specs=[hbm] * 5,
-        out_specs=(hbm, pl.BlockSpec(memory_space=VMEM)),
+        out_specs=(pl.BlockSpec(memory_space=VMEM),) * 2,
         scratch_shapes=[
             pltpu.SMEM(flags.shape, jnp.int32),
             scratch((6,) + plane),
@@ -491,20 +494,18 @@
             scratch((14, 2, FACE + 2 * PAD, FACE)),
             scratch((6,) + plane),
             scratch((3,) + plane),
-            scratch((6,) + plane),
             scratch((2, 6) + plane),
             scratch((2, 3, 8, 8, FACE)),
         ]
         + [scratch((2,) + plane)] * 12
-        + [dma((6,)), dma((2, 6)), dma((2, 6)), dma((2, 3, 8)), dma((2, 3, 8))],
+        + [dma((5,)), dma((2, 6)), dma((2, 6)), dma((2, 3, 8)), dma((2, 3, 8))],
         compiler_params=pltpu.CompilerParams(collective_id=1, has_side_effects=True),
         cost_estimate=pl.CostEstimate(
             flops=80_000_000, bytes_accessed=4_000_000, transcendentals=800_000
         ),
         name="section",
     )(flags, section_state[0, 0], volume[0, 0], distance[0, 0], base_state[0, 0])
-    cells = lax.axis_size("comp") * lax.axis_size("blk") * 2 * FACE * FACE
-    return new[None, None], jnp.sqrt(total[0, 0] / cells)
+    return new[None, None], total[0, 0]
 
 
 def solution(mesh):

time: 50.5 us -> 47.9 us (0.949)
  local copies, waits for them, and re-layouts: 2.06 us -> 0.88 us
  Pallas kernels: 45.7 us -> 44.6 us
    unnamed x1, local copies, waits for them, and re-layouts: 2.06 us -> 0.88 us
    pallas_call x1, Pallas kernels: 45.7 us -> 44.6 us  [per_device(): pl.pallas_call(entry, out_shape=(scratch((6,) + plane), f32((1, 1))), in_...]
where the time goes in v4:
time: 47.9 us; the launch traced here: 47.8 us
  Pallas kernels  44.6 us (93%)
  between operations  2.33 us (5%)
  local copies, waits for them, and re-layouts  0.88 us (2%)
    pallas_call x1, Pallas kernels, per_device(): pl.pallas_call(entry, out_shape=(scratch((6,) + plane), f32((1, 1))), in_...  44.6 us

profile of v4, /device:TPU:1, one launch (start us, length us, event | category | flops | bytes accessed | tf_op | source)
XLA Modules:
  0.0 47.8 jit_solution(153691069538030834)
XLA Ops:
  0.6 44.6 %section.1 = (f32[6,2,128,128]{3,2,1,0:T(8,128)S(1)}, f32[1,1]{1,0:T(1,128)}) custom-call(s32[3,8,64]{2,1,0:T(8,128)} %bitcast.12, f32[6,2,128,128]{3,2,1,0:T(8,128)} %bitcast.8, f32[2,128,128]{2,1,0:T(8,128)} %bitcast.10, f32[2,128,128]{2,1,0:T(8,128)} %bitcast.11, f32[6,2,128,128]{3,2,1,0:T(8,128)} %bitcast.9), custom_call_target="tpu_custom_call" | custom-call | flops 80000000 | bytes 4000000 | tf_op jit(solution)/shard_map/section/pallas_call | solution.py:483
  45.2 0.9 %copy.9 = f32[1,1,6,2,128,128]{5,4,3,2,1,0:T(8,128)} copy(f32[1,1,6,2,128,128]{5,4,3,2,1,0:T(8,128)S(1)} %bitcast.7) | data formatting | bytes 1572864

commit v5 on v4

--- a/solution.py
+++ b/solution.py
@@ -144,8 +144,8 @@
         return pltpu.make_async_remote_copy(
             src_ref=slots.at[kind, n, me],
             dst_ref=slots.at[kind, n, me],
-            send_sem=rsend.at[kind, n, step],
-            recv_sem=rrecv.at[kind, n, me],
+            send_sem=rsend.at[kind, n],
+            recv_sem=rrecv.at[kind, n],
             device_id=device((me + step) % 8),
             device_id_type=MESH,
         )
@@ -156,22 +156,11 @@
             exchange(kind, n, step).start()
 
     def receive(kind, n, op):
-        me, device = phases[n]
-        for step in range(1, 8):
-            other = (me + step) % 8
-            pltpu.make_async_remote_copy(
-                src_ref=slots.at[kind, n, me],
-                dst_ref=slots.at[kind, n, other],
-                send_sem=rsend.at[kind, n, step],
-                recv_sem=rrecv.at[kind, n, other],
-                device_id=device(other),
-                device_id_type=MESH,
-            ).wait_recv()
+        seven = slots.at[kind, n, pl.ds(0, 7)]
+        pltpu.make_async_copy(seven, seven, rrecv.at[kind, n]).wait()
         held = slots[kind, n, 0]
         for j in range(1, 8):
             held = op(held, slots[kind, n, j])
-        for step in range(1, 8):
-            exchange(kind, n, step).wait_send()
         return held
 
     sides = ((has_below, has_above, above_id), (has_above, has_below, below_id))
@@ -179,7 +168,7 @@
     def halo_copy(side, f):
         return pltpu.make_async_remote_copy(
             src_ref=state_hbm.at[f],
-            dst_ref=halo[side][f].at[0],
+            dst_ref=halo[side][f],
             send_sem=hsend.at[side, f],
             recv_sem=hrecv.at[side, f],
             device_id=sides[side][2],
@@ -214,9 +203,11 @@
         return least
 
     def fill(k, least):
-        return fill_rows(2 * k + 1, fill_rows(2 * k, least))
-
-    limit = lax.fori_loop(0, STEPS // 2, fill, jnp.full((ROWS, FACE), jnp.inf, jnp.float32))
+        for i in range(4):
+            least = fill_rows(4 * k + i, least)
+        return least
+
+    limit = lax.fori_loop(0, STEPS // 4, fill, jnp.full((ROWS, FACE), jnp.inf, jnp.float32))
     for layer in range(2):
         for i in range(14):
             first_row = wide[i, layer, PAD : PAD + 1, :]
@@ -240,7 +231,7 @@
     def before(x):
         return jnp.where(first, x, pltpu.roll(x, 1, 1))
 
-    def local_flux(layer, fields, vorticity, low, high, carry=None):
+    def local_rows(layer, fields, vorticity):
         def load(i, k, offset):
             return wide[i, layer, pl.ds(k * ROWS + PAD + offset, ROWS), :]
 
@@ -286,14 +277,26 @@
                 vort[2, layer, at, :] = d2u0
             return tuple(turned)
 
-        if carry is None:
+        def start():
             w0, q0 = states(0, 0), cell(0, 0)
             s0 = sensor(load(9, 0, -1), q0["p"], load(9, 0, 1))
-            carry = edge_flux(2, w0, states(0, 1), q0, s0, fields)
-        return lax.fori_loop(low, high, body, tuple(carry))
-
-    for layer in range(2):
-        local_flux(layer, (0,), False, 0, STEPS)
+            return tuple(edge_flux(2, w0, states(0, 1), q0, s0, fields))
+
+        return body, start
+
+    def local_flux(fields, vorticity, low, high, group, carry=None):
+        layers = [local_rows(layer, fields, vorticity) for layer in range(2)]
+
+        def body(k, carry):
+            for i in range(group):
+                carry = tuple(layers[l][0](group * k + i, carry[l]) for l in range(2))
+            return carry
+
+        if carry is None:
+            carry = tuple(start() for _, start in layers)
+        return lax.fori_loop(low // group, high // group, body, carry)
+
+    local_flux((0,), False, 0, STEPS, 2)
 
     def one_if(condition):
         return jnp.where(condition, 1, 0)
@@ -321,36 +324,25 @@
                 @pl.when(jnp.logical_not(sides[side][0]))
                 def _():
                     for layer in range(2):
-                        halo[side][f][0, layer] = state[f, side]
+                        halo[side][f][layer] = state[f, side]
 
         for side in range(2):
+            (turn, reverse_rows, reverse_lanes), signs = turns[side]
             for f in fields:
                 for layer in range(2):
-                    source = halo[side][{2: 3, 3: 2}.get(f, f)]
-                    halo[side][f][1, layer] = source[0, layer].T
-
-        def place(k, _):
-            pair = (rows_of(k), rows_of(STEPS - 1 - k))
-            for side in range(2):
-                (turn, reverse_rows, reverse_lanes), signs = turns[side]
-                for f in fields:
-                    buf = halo[side][f]
-                    for layer in range(2):
-                        x = [
-                            jnp.where(turn, buf[1, layer, at, :], buf[0, layer, at, :])
-                            for at in pair
-                        ]
-                        flipped = [jnp.take_along_axis(y, ROWS - 1 - row, axis=0) for y in x]
-                        for i in range(2):
-                            y = jnp.where(reverse_rows, flipped[1 - i], x[i])
-                            z = jnp.take_along_axis(y, FACE - 1 - lane, axis=1)
-                            y = jnp.where(reverse_lanes, z, y)
-                            if f in (2, 3):
-                                y = y * signs[f - 2]
-                            ghost[side, f, layer, pair[i], :] = y
-            return 0
-
-        lax.fori_loop(0, STEPS // 2, place, 0)
+                    turned = halo[side][{2: 3, 3: 2}.get(f, f)][layer].T
+                    x = []
+                    for k in range(STEPS):
+                        at = slice(k * ROWS, (k + 1) * ROWS)
+                        x.append(jnp.where(turn, turned[at], halo[side][f][layer, at, :]))
+                    for k in range(STEPS):
+                        y = jnp.take_along_axis(x[STEPS - 1 - k], ROWS - 1 - row, axis=0)
+                        y = jnp.where(reverse_rows, y, x[k])
+                        z = jnp.take_along_axis(y, FACE - 1 - lane, axis=1)
+                        y = jnp.where(reverse_lanes, z, y)
+                        if f in (2, 3):
+                            y = y * signs[f - 2]
+                        ghost[side, f, layer, k * ROWS : (k + 1) * ROWS, :] = y
 
     arrive(ORDER[0])
     arrive(ORDER[1])
@@ -441,10 +433,9 @@
         return 0
 
     others = (1, 2, 3, 4, 5)
-    held = local_flux(0, others, True, 0, 4)
+    held = local_flux(others, True, 0, 2, 1)
     send(1, 1, receive(1, 0, jnp.add))
-    local_flux(0, others, True, 4, STEPS, held)
-    local_flux(1, others, True, 0, STEPS)
+    local_flux(others, True, 2, STEPS, 1, held)
     send(1, 2, receive(1, 1, jnp.add))
     least = receive(0, 2, jnp.minimum)
     least = jnp.broadcast_to(jnp.min(least, axis=(0, 1), keepdims=True), (ROWS, FACE))
@@ -458,6 +449,10 @@
             def _():
                 halo_copy(side, f).wait_send()
 
+    for kind in range(2):
+        for n in range(3):
+            seven = slots.at[kind, n, pl.ds(0, 7)]
+            pltpu.make_async_copy(seven, seven, rsend.at[kind, n]).wait()
     cells = lax.axis_size("comp") * chain * 2 * FACE * FACE
     norm = jnp.sum(receive(1, 2, jnp.add), axis=(0, 1), keepdims=True)
     total_out[...] = jnp.sqrt(norm / cells)
@@ -497,8 +492,8 @@
             scratch((2, 6) + plane),
             scratch((2, 3, 8, 8, FACE)),
         ]
-        + [scratch((2,) + plane)] * 12
-        + [dma((5,)), dma((2, 6)), dma((2, 6)), dma((2, 3, 8)), dma((2, 3, 8))],
+        + [scratch(plane)] * 12
+        + [dma((5,)), dma((2, 6)), dma((2, 6)), dma((2, 3)), dma((2, 3))],
         compiler_params=pltpu.CompilerParams(collective_id=1, has_side_effects=True),
         cost_estimate=pl.CostEstimate(
             flops=80_000_000, bytes_accessed=4_000_000, transcendentals=800_000

time: 47.9 us -> 43.5 us (0.908)
  the two profiles are of different devices: /device:TPU:1 before, /device:TPU:64 now
where the time goes in v5:
time: 43.5 us; the launch traced here: 43.4 us
  Pallas kernels  40.2 us (92%)
  between operations  2.33 us (5%)
  local copies, waits for them, and re-layouts  0.88 us (2%)
    pallas_call x1, Pallas kernels, per_device(): pl.pallas_call(entry, out_shape=(scratch((6,) + plane), f32((1, 1))), in_...  40.2 us
    unnamed x1, local copies, waits for them, and re-layouts  0.88 us

profile of v5, /device:TPU:64, one launch (start us, length us, event | category | flops | bytes accessed | tf_op | source)
XLA Modules:
  0.0 43.4 jit_solution(3680833676913418652)
XLA Ops:
  0.6 40.2 %section.1 = (f32[6,2,128,128]{3,2,1,0:T(8,128)S(1)}, f32[1,1]{1,0:T(1,128)}) custom-call(s32[3,8,64]{2,1,0:T(8,128)} %bitcast.12, f32[6,2,128,128]{3,2,1,0:T(8,128)} %bitcast.8, f32[2,128,128]{2,1,0:T(8,128)} %bitcast.10, f32[2,128,128]{2,1,0:T(8,128)} %bitcast.11, f32[6,2,128,128]{3,2,1,0:T(8,128)} %bitcast.9), custom_call_target="tpu_custom_call" | custom-call | flops 80000000 | bytes 4000000 | tf_op jit(solution)/shard_map/section/pallas_call | solution.py:478
  40.8 0.9 %copy.9 = f32[1,1,6,2,128,128]{5,4,3,2,1,0:T(8,128)} copy(f32[1,1,6,2,128,128]{5,4,3,2,1,0:T(8,128)S(1)} %bitcast.7) | data formatting | bytes 1572864

commit v6 on v5

--- a/solution.py
+++ b/solution.py
@@ -217,7 +217,7 @@
             wide[i, layer, PAD + FACE : PAD + FACE + 1, :] = last_row
             wide[i, layer, PAD + FACE + 1 : PAD + FACE + 2, :] = last_row
 
-    send(0, 0, limit)
+    send(0, 0, jnp.min(limit, axis=0, keepdims=True))
     for fields in ORDER[1:]:
         send_halo(fields)
 
@@ -391,7 +391,7 @@
         return density_rows(2 * k + 1, density_rows(2 * k, total))
 
     total = lax.fori_loop(0, STEPS // 2, density, jnp.zeros((ROWS, FACE), jnp.float32))
-    send(1, 0, total)
+    send(1, 0, jnp.sum(total, axis=0, keepdims=True))
     send(0, 2, receive(0, 1, jnp.minimum))
     arrive(ORDER[4])
 
@@ -490,7 +490,7 @@
             scratch((6,) + plane),
             scratch((3,) + plane),
             scratch((2, 6) + plane),
-            scratch((2, 3, 8, 8, FACE)),
+            scratch((2, 3, 8, 1, FACE)),
         ]
         + [scratch(plane)] * 12
         + [dma((5,)), dma((2, 6)), dma((2, 6)), dma((2, 3)), dma((2, 3))],

time: 43.5 us -> 41.9 us (0.963)
  the two profiles are of different devices: /device:TPU:64 before, /device:TPU:2 now
where the time goes in v6:
time: 41.9 us; the launch traced here: 41.8 us
  Pallas kernels  38.6 us (92%)
  between operations  2.33 us (6%)
  local copies, waits for them, and re-layouts  0.88 us (2%)
    pallas_call x1, Pallas kernels, per_device(): pl.pallas_call(entry, out_shape=(scratch((6,) + plane), f32((1, 1))), in_...  38.6 us
    unnamed x1, local copies, waits for them, and re-layouts  0.88 us

profile of v6, /device:TPU:2, one launch (start us, length us, event | category | flops | bytes accessed | tf_op | source)
XLA Modules:
  0.0 41.8 jit_solution(3401113564673675841)
XLA Ops:
  0.6 38.6 %section.1 = (f32[6,2,128,128]{3,2,1,0:T(8,128)S(1)}, f32[1,1]{1,0:T(1,128)}) custom-call(s32[3,8,64]{2,1,0:T(8,128)} %bitcast.12, f32[6,2,128,128]{3,2,1,0:T(8,128)} %bitcast.8, f32[2,128,128]{2,1,0:T(8,128)} %bitcast.10, f32[2,128,128]{2,1,0:T(8,128)} %bitcast.11, f32[6,2,128,128]{3,2,1,0:T(8,128)} %bitcast.9), custom_call_target="tpu_custom_call" | custom-call | flops 80000000 | bytes 4000000 | tf_op jit(solution)/shard_map/section/pallas_call | solution.py:478
  39.2 0.9 %copy.9 = f32[1,1,6,2,128,128]{5,4,3,2,1,0:T(8,128)} copy(f32[1,1,6,2,128,128]{5,4,3,2,1,0:T(8,128)S(1)} %bitcast.7) | data formatting | bytes 1572864

commit v7 on v6

--- a/solution.py
+++ b/solution.py
@@ -120,17 +120,17 @@
         copy.start()
 
     barrier = pltpu.get_barrier_semaphore()
+    for me, device in phases[::-1]:
+        for step in (4, 3, 5, 2, 6, 1, 7):
+            pl.semaphore_signal(
+                barrier, inc=1, device_id=device((me + step) % 8), device_id_type=MESH
+            )
     for has, device in ((has_below, below_id), (has_above, above_id)):
 
         @pl.when(has)
         def _():
             pl.semaphore_signal(barrier, inc=1, device_id=device, device_id_type=MESH)
 
-    for me, device in phases:
-        for step in range(1, 8):
-            pl.semaphore_signal(
-                barrier, inc=1, device_id=device((me + step) % 8), device_id_type=MESH
-            )
 
     def rows_of(k):
         return pl.ds(pl.multiple_of(k * ROWS, ROWS), ROWS)
@@ -152,7 +152,7 @@
 
     def send(kind, n, value):
         slots[kind, n, pl.ds(phases[n][0], 1)] = value[None]
-        for step in range(1, 8):
+        for step in (4, 3, 5, 2, 6, 1, 7):
             exchange(kind, n, step).start()
 
     def receive(kind, n, op):
@@ -348,6 +348,20 @@
     arrive(ORDER[1])
     send(0, 1, receive(0, 0, jnp.minimum))
     arrive(ORDER[2])
+
+    def prepare(k, _):
+        for at in (rows_of(2 * k), rows_of(2 * k + 1)):
+            for side in range(2):
+                for layer in range(2):
+                    w = [ghost[side, f, layer, at, :] for f in range(4)]
+                    inv = 1.0 / w[0]
+                    kinetic = w[1] * (w[1] * inv) + w[2] * (w[2] * inv) + w[3] * (w[3] * inv)
+                    ghost[side, 6, layer, at, :] = 0.5 * kinetic
+                    ghost[side, 7, layer, at, :] = w[1] * inv
+                    ghost[side, 8, layer, at, :] = inv
+        return 0
+
+    lax.fori_loop(0, STEPS // 2, prepare, 0)
     arrive(ORDER[3])
 
     def own(i, layer, k):
@@ -363,12 +377,11 @@
                 p.append(own(9, layer, k))
                 cs.append(own(10, layer, k))
             else:
-                w = [ghost[side, f, layer, at, :] for f in range(5)]
-                q = primitives(w + [w[0]])
-                rho.append(w[0])
-                un.append(q["u"][0])
-                p.append(q["p"])
-                cs.append(q["cs"])
+                energy, kinetic = ghost[side, 4, layer, at, :], ghost[side, 6, layer, at, :]
+                rho.append(ghost[side, 0, layer, at, :])
+                un.append(ghost[side, 7, layer, at, :])
+                p.append(0.4 * (energy - kinetic))
+                cs.append(jnp.sqrt(GAMMA * (p[-1] * ghost[side, 8, layer, at, :])))
         s = [None] + [sensor(p[i - 1], p[i], p[i + 1]) for i in range(1, 5)]
         g = []
         for i in range(1, 4):
@@ -489,7 +502,7 @@
             scratch((14, 2, FACE + 2 * PAD, FACE)),
             scratch((6,) + plane),
             scratch((3,) + plane),
-            scratch((2, 6) + plane),
+            scratch((2, 9) + plane),
             scratch((2, 3, 8, 1, FACE)),
         ]
         + [scratch(plane)] * 12

time: 41.9 us -> 41.5 us (level)
  no operation moved by 1% of the time
where the time goes in v7:
time: 41.5 us; the launch traced here: 41.4 us
  Pallas kernels  38.2 us (92%)
  between operations  2.33 us (6%)
  local copies, waits for them, and re-layouts  0.88 us (2%)
    pallas_call x1, Pallas kernels, per_device(): pl.pallas_call(entry, out_shape=(scratch((6,) + plane), f32((1, 1))), in_...  38.2 us
    unnamed x1, local copies, waits for them, and re-layouts  0.88 us

profile of v7, /device:TPU:2, one launch (start us, length us, event | category | flops | bytes accessed | tf_op | source)
XLA Modules:
  0.0 41.4 jit_solution(9922629125061805064)
XLA Ops:
  0.6 38.2 %section.1 = (f32[6,2,128,128]{3,2,1,0:T(8,128)S(1)}, f32[1,1]{1,0:T(1,128)}) custom-call(s32[3,8,64]{2,1,0:T(8,128)} %bitcast.12, f32[6,2,128,128]{3,2,1,0:T(8,128)} %bitcast.8, f32[2,128,128]{2,1,0:T(8,128)} %bitcast.10, f32[2,128,128]{2,1,0:T(8,128)} %bitcast.11, f32[6,2,128,128]{3,2,1,0:T(8,128)} %bitcast.9), custom_call_target="tpu_custom_call" | custom-call | flops 80000000 | bytes 4000000 | tf_op jit(solution)/shard_map/section/pallas_call | solution.py:491
  38.8 0.9 %copy.9 = f32[1,1,6,2,128,128]{5,4,3,2,1,0:T(8,128)} copy(f32[1,1,6,2,128,128]{5,4,3,2,1,0:T(8,128)S(1)} %bitcast.7) | data formatting | bytes 1572864
